TPU v7x, 512 devices: a whole 4x8x8 slice. The times are simulated.
512 devices in a mesh: pair: 32 (over x, y), ph: 16 (over z, core).
Axes of the slice: x: 4, y: 8, z: 8, core: 2. Of those that a mesh axis runs over, the one named last changes fastest.
Arguments:
- t_cycle: float32 [8, 512, 8192], P(None, 'pair', 'ph'), may hold values from -6 to 6
- w_cycle: float32 [8, 8192, 4096], P(None, 'ph', 'pair'), may hold values from -0.1875 to 0.1875
- occ_energy: float32 [64], replicated, may hold values from -1.5 to -0.5
- vir_energy: float32 [8, 128], replicated, may hold values from 0.2 to 1.5
- occ_irrep: int32 [64], replicated, may hold values from 0 to 7
- vir_count: int32 [8], replicated, may hold values from 1 to 128, 640 in all
Outputs:
- increment: float32 [8, 512, 4096], P(None, 'ph', 'pair')
Inputs may be any that keep to these rules, and one draw needn't show every extreme that they name: `occ_irrep`: irrep labels combine by exclusive or. `vir_count`: the counts sum to 640; one irrep fills all 128 slots.
All inputs are finite; a program needn't handle non-finite values.
Results may differ from a plain program's by a relative error of at most 0.000075.
Values sent between devices are 32-bit elements; how exact they have to be, the bound alone decides.
No kernel may reach another device: no remote copies, remote signals or barrier semaphores. Data moves between devices by JAX's collectives and lax.ppermute only.
A program may use at most 64 MiB of HBM per device.

v0:
```python
import jax
import jax.numpy as jnp
from jax import lax
from jax.sharding import PartitionSpec as P

IRREPS = 8
VIRT_CAP = 128
ROW_OCC = 4
COL_OCC = 32
ROWS = 512
PAIRS = 8192
COLS = 4096


def reduce_rows(partial_value):
    return lax.psum_scatter(partial_value, "ph", scatter_dimension=1, tiled=True)


def on_device(t_cycle, w_cycle, occ_energy, vir_energy, occ_irrep, vir_count):
    n_pair = lax.axis_size("pair")
    n_ph = lax.axis_size("ph")
    ph_index = lax.axis_index("ph")
    pair_index = lax.axis_index("pair")
    local_rows = t_cycle.shape[1]
    local_pairs = t_cycle.shape[2]
    local_cols = w_cycle.shape[2]
    out_rows = local_rows * n_pair // n_ph
    slot_ids = jnp.arange(VIRT_CAP, dtype=jnp.int32)
    irreps = jnp.arange(IRREPS, dtype=jnp.int32)
    symmetry = jnp.bitwise_xor(occ_irrep[None, :], irreps[:, None])
    onehot = symmetry[:, :, None] == irreps[None, None, :]
    counts = jnp.sum(jnp.where(onehot, vir_count[None, None, :], 0), axis=2)
    live_slot = (slot_ids[None, None, :] < counts[:, :, None]).astype(jnp.float32)
    vir_ener = jnp.einsum(
        "goh,hv->gov",
        onehot.astype(jnp.float32),
        vir_energy,
        precision=lax.Precision.HIGHEST,
        preferred_element_type=jnp.float32,
    )
    mask_pair = lax.dynamic_slice_in_dim(
        live_slot.reshape(IRREPS, PAIRS), ph_index * local_pairs, local_pairs, 1
    )
    w_masked = w_cycle * mask_pair[:, :, None]
    mask_row = lax.dynamic_slice_in_dim(
        live_slot[:, :ROW_OCC].reshape(IRREPS, ROWS), ph_index * out_rows, out_rows, 1
    )
    mask_col = lax.dynamic_slice_in_dim(
        live_slot[:, :COL_OCC].reshape(IRREPS, COLS), pair_index * local_cols, local_cols, 1
    )
    e_row = (occ_energy[None, :ROW_OCC, None] - vir_ener[:, :ROW_OCC]).reshape(IRREPS, ROWS)
    e_col = (occ_energy[None, :COL_OCC, None] - vir_ener[:, :COL_OCC]).reshape(IRREPS, COLS)
    e_row = lax.dynamic_slice_in_dim(e_row, ph_index * out_rows, out_rows, 1)
    e_col = lax.dynamic_slice_in_dim(e_col, pair_index * local_cols, local_cols, 1)
    partial_value = jnp.einsum(
        "grk,gkc->grc",
        lax.all_gather(t_cycle, "pair", axis=1, tiled=True),
        w_masked,
        precision=lax.Precision.HIGHEST,
        preferred_element_type=jnp.float32,
    )
    summed = reduce_rows(partial_value)
    return (
        mask_row[:, :, None]
        * mask_col[:, None, :]
        * summed
        / (e_row[:, :, None] + e_col[:, None, :])
    )


def solution(mesh):
    return jax.shard_map(
        on_device,
        mesh=mesh,
        in_specs=(P(None, "pair", "ph"), P(None, "ph", "pair"), P(), P(), P(), P()),
        out_specs=P(None, "ph", "pair"),
        check_vma=False,
    )
```

profile of v0, /device:TPU:1, one launch (start us, length us, event | category | flops | bytes accessed | tf_op | source)
XLA Modules:
  0.0 200.1 jit_solution(11864317667957786671)
XLA Ops:
  6.5 0.0 copy-start
  6.5 0.0 all-gather.2.cloned.1.call-start
  6.5 0.7 all-gather.2.cloned.1.call-update
  7.3 0.0 reduce-scatter.2.cloned.1.call-start
  7.3 0.7 iota_xor_fusion
  8.0 0.7 select_reduce_fusion
  8.7 0.1 copy.9
  8.8 0.1 dynamic-slice
  8.9 0.1 broadcast_bitcast_fusion
  9.0 109.2 %all-gather.2.cloned.1.call-done = f32[8,512,512]{2,1,0:T(8,128)} async-done(((f32[8,16,512]{2,1,0:T(8,128)}), f32[8,512,512]{2,1,0:T(8,128)}) %all-gather.2.cloned.1.call-update) | async-done | bytes 8388624 | tf_op jit(solution)/shard_map/all_gather | solution.py:57
  118.2 12.4 %fusion.2 = f32[8,512,128]{1,2,0:T(8,128)S(1)} fusion(f32[8,512,512]{2,1,0:T(8,128)} %all-gather.2.cloned.1.call-done, f32[8,512,128]{2,1,0:T(8,128)} %param.7, f32[8,512]{1,0:T(8,128)S(1)} %fusion.11), kind=kOutput, calls=%fused_computation.2 | convolution fusion | flops 3221749760 | bytes 12599296 | tf_op jit(solution)/shard_map/grk,gkc->grc/dot_general | solution.py:55
  130.6 1.9 copy.12
  132.5 0.0 copy-start.1
  132.5 0.0 reduce-scatter.2.cloned.1.call-update
  132.5 0.1 fusion.6
  132.6 0.1 copy.10
  132.8 0.0 copy-done
  132.8 0.4 fusion.8
  133.2 0.0 copy-done.1
  133.2 0.1 fusion.7
  133.3 0.1 copy.20
  133.4 0.1 fusion.9
  133.5 0.1 constant_dynamic-slice_fusion
  133.5 0.1 copy.13
  133.7 57.8 %reduce-scatter.2.cloned.1.call-done = f32[8,32,128]{2,0,1:T(8,128)} async-done(((f32[8,512,128]{2,0,1:T(8,128)}), f32[8,32,128]{2,0,1:T(8,128)}) %reduce-scatter.2.cloned.1.call-update) | async-done | bytes 131088 | tf_op jit(solution)/shard_map/reduce_scatter | solution.py:16
  191.5 1.0 add_divide_fusion
  192.5 0.7 copy.14
  (7 shorter events, 0.1 us)
Async XLA Ops:
  6.5 126.2 %copy-start = (f32[8,128]{1,0:T(8,128)S(1)}, f32[8,128]{1,0:T(8,128)}, u32[]{:S(2)}) copy-start(f32[8,128]{1,0:T(8,128)} %param.9) | copy-start | bytes 12292
  6.5 111.7 %all-gather.2.cloned.1.call-start = ((), (), s32[]{:S(2)}) async-start(), calls=%async_computation.1 | async-start | bytes 8650752 | tf_op jit(solution)/shard_map/all_gather | solution.py:57
  7.3 184.2 %reduce-scatter.2.cloned.1.call-start = ((), (), s32[]{:S(2)}) async-start(), calls=%async_computation.2 | async-start | bytes 2228224 | tf_op jit(solution)/shard_map/reduce_scatter | solution.py:16
  132.5 0.7 copy-start.1
Sparse Core Ops, SparseCore 0:
  10.5 107.6 all-gather.1
  132.6 58.8 reduce-scatter.1
where the time goes:
time: 202 us; the launch traced here: 200 us
  waiting for transfers between devices  168 us (83%)
  between operations  13.5 us (7%)
  matrix products  12.8 us (6%)
  local copies, waits for them, and re-layouts  3.24 us (2%)
  other arithmetic  2.73 us (1%)
    all_gather x1, waiting for transfers between devices, on_device(): lax.all_gather(t_cycle, 'pair', axis=1, tiled=True)  109 us
    reduce_scatter x1, waiting for transfers between devices, reduce_rows(): lax.psum_scatter(partial_value, 'ph', scatter_dimension=1, tiled=True)  57.8 us
    dot_general x1, matrix products, on_device(): jnp.einsum('grk,gkc->grc', lax.all_gather(t_cycle, 'pair', axis=1, tiled=...  12.4 us
  transfers between devices with their start and end apart: 2, of which 2 were waited for; matrix products, arithmetic and copies ran while one was open for 1% of the time, Pallas kernels for 0%

commit v1 on v0

v1 whole, which is shorter than its diff:
```python
import jax
import jax.numpy as jnp
import numpy as np
from jax import lax
from jax.experimental import pallas as pl
from jax.experimental.pallas import tpu as pltpu
from jax.sharding import Mesh, PartitionSpec as P

IRREPS = 8
SLOTS = 128
NX, NY, NZ, NC = 4, 8, 8, 2
AXES = ("x", "y", "z", "c")
K_LOCAL = 512
OFFSETS = (0, 1, 7, 4, 2, 5, 6, 3)


def shift_y(value, step):
    ids = np.arange(NX * NY * NZ * NC).reshape(NX, NY, NZ, NC)
    targets = np.roll(ids, -step, axis=1)
    return lax.ppermute(value, AXES, list(zip(ids.ravel().tolist(), targets.ravel().tolist())))


def split(value):
    high = value.astype(jnp.bfloat16)
    low = (value - high.astype(jnp.float32)).astype(jnp.bfloat16)
    return high, low


def product_body(occ_ref, count_ref, t0, t1, t2, t3, t45, t67, w_ref, out_ref, t_high, t_low, w_high, w_low):
    y = lax.axis_index("y")
    z = lax.axis_index("z")
    g = lax.axis_index("x") * NC + lax.axis_index("c")

    @pl.when(pl.program_id(0) == 0)
    def _():
        blocks = [(t0, 0), (t1, 0), (t2, 0), (t3, 0), (t45, 0), (t45, 8), (t67, 0), (t67, 8)]
        for slot, (ref, first) in enumerate(blocks):
            for i in range(NX):
                for c in range(NC):
                    high, low = split(ref[first + i * NC + c])
                    rows = pl.ds((slot * NX + i) * 16, 16)
                    cols = pl.ds(c * K_LOCAL, K_LOCAL)
                    t_high[rows, cols] = high
                    t_low[rows, cols] = low

    slots = lax.broadcasted_iota(jnp.int32, (SLOTS, SLOTS), 0)
    for c in range(NC):
        for k in range(4):
            live = slots < count_ref[jnp.bitwise_xor(occ_ref[z * 8 + c * 4 + k], g)]
            for half in range(2):
                part = jnp.where(live, w_ref[half * NC + c, pl.ds(k * SLOTS, SLOTS), :], 0.0)
                high, low = split(part)
                rows = pl.ds(c * K_LOCAL + k * SLOTS, SLOTS)
                cols = pl.ds(half * SLOTS, SLOTS)
                w_high[rows, cols] = high
                w_low[rows, cols] = low

    def dot(a, b):
        return jnp.dot(a[...], b[...], preferred_element_type=jnp.float32)

    total = dot(t_high, w_low) + dot(t_low, w_high) + dot(t_high, w_high)
    for slot, offset in enumerate(OFFSETS):
        first = pl.multiple_of(lax.rem(y + offset, NY) * 16, 16)
        for i in range(NX):
            for half in range(2):
                rows = slice((slot * NX + i) * 16, (slot * NX + i + 1) * 16)
                out_ref[half, i, pl.ds(first, 16), :] = total[rows, half * SLOTS : (half + 1) * SLOTS]


def product(occ_irrep, vir_count, blocks, w):
    whole = lambda shape: pl.BlockSpec(shape, lambda n: (0,) * len(shape))
    return pl.pallas_call(
        product_body,
        grid=(2,),
        in_specs=[
            pl.BlockSpec(memory_space=pltpu.SMEM),
            pl.BlockSpec(memory_space=pltpu.SMEM),
            *[whole(b.shape) for b in blocks],
            pl.BlockSpec((4, K_LOCAL, SLOTS), lambda n: (n, 0, 0)),
        ],
        out_specs=pl.BlockSpec((2, NX, SLOTS, SLOTS), lambda n: (n, 0, 0, 0)),
        out_shape=jax.ShapeDtypeStruct((NX, NX, SLOTS, SLOTS), jnp.float32),
        scratch_shapes=[
            pltpu.VMEM((512, 2 * K_LOCAL), jnp.bfloat16),
            pltpu.VMEM((512, 2 * K_LOCAL), jnp.bfloat16),
            pltpu.VMEM((2 * K_LOCAL, 2 * SLOTS), jnp.bfloat16),
            pltpu.VMEM((2 * K_LOCAL, 2 * SLOTS), jnp.bfloat16),
        ],
        name="product",
    )(occ_irrep, vir_count, *blocks, w)


def finish_body(parts_ref, factor_ref, out_ref):
    for x in range(NX):
        for c in range(NC):
            total = parts_ref[x, 0, c]
            for z in range(1, NZ):
                total = total + parts_ref[x, z, c]
            out_ref[x * NC + c] = total * factor_ref[x * NC + c]


def finish(parts, factor):
    return pl.pallas_call(
        finish_body,
        out_shape=jax.ShapeDtypeStruct((IRREPS, 32, SLOTS), jnp.float32),
        name="finish",
    )(parts, factor)


def factors(occ_energy, vir_energy, occ_irrep, vir_count):
    row_i = lax.axis_index("z") // 2
    row_a = (lax.axis_index("z") % 2 * NC + lax.axis_index("c")) * 32
    col_j = lax.axis_index("x") * NY + lax.axis_index("y")
    irreps = jnp.arange(IRREPS, dtype=jnp.int32)
    slots = jnp.arange(SLOTS, dtype=jnp.int32)

    def side(occupied):
        label = jnp.bitwise_xor(lax.dynamic_index_in_dim(occ_irrep, occupied, 0, False), irreps)
        onehot = label[:, None] == irreps[None, :]
        count = jnp.sum(jnp.where(onehot, vir_count[None, :], 0), axis=1)
        energy = jnp.sum(jnp.where(onehot[:, :, None], vir_energy[None], 0.0), axis=1)
        energy = lax.dynamic_index_in_dim(occ_energy, occupied, 0, False) - energy
        return energy, (slots[None, :] < count[:, None]).astype(jnp.float32)

    e_row, m_row = side(row_i)
    e_col, m_col = side(col_j)
    e_row = lax.dynamic_slice_in_dim(e_row, row_a, 32, 1)
    m_row = lax.dynamic_slice_in_dim(m_row, row_a, 32, 1)
    return m_row[:, :, None] * m_col[:, None, :] / (e_row[:, :, None] + e_col[:, None, :])


def on_device(t_cycle, w_cycle, occ_energy, vir_energy, occ_irrep, vir_count):
    own = lax.all_to_all(t_cycle, ("x", "c"), 0, 0, tiled=True)
    w_cycle, own = lax.optimization_barrier((w_cycle, own))
    up = shift_y(own, -1)
    down = shift_y(own, 1)
    across = shift_y(own, 4)
    w = lax.all_to_all(w_cycle, ("x", "c"), 0, 0, tiled=True)
    up_pair = shift_y(jnp.concatenate([up, across], axis=0), -1)
    down_pair = shift_y(jnp.concatenate([down, across], axis=0), 1)
    blocks = (own, up, down, across, up_pair, down_pair)
    partial = product(occ_irrep, vir_count, blocks, w)
    parts = lax.all_to_all(partial.reshape(NX * NZ * NC, 32, SLOTS), ("x", "z", "c"), 0, 0, tiled=True)
    factor = factors(occ_energy, vir_energy, occ_irrep, vir_count)
    return finish(parts.reshape(NX, NZ, NC, 32, SLOTS), factor)


def solution(mesh):
    grid = Mesh(mesh.devices.reshape(NX, NY, NZ, NC), AXES)
    return jax.shard_map(
        on_device,
        mesh=grid,
        in_specs=(P(None, ("x", "y"), ("z", "c")), P(None, ("z", "c"), ("x", "y")), P(), P(), P(), P()),
        out_specs=P(None, ("z", "c"), ("x", "y")),
        check_vma=False,
    )
```

time: 202 us -> 117 us (0.58)
  waiting for transfers between devices: 168 us -> 51 us
  starting transfers between devices: 0.04 us -> 33.2 us
  blocking collectives: 0 us -> 16.6 us
  between operations: 13.5 us -> 0.2 us
  matrix products: 12.8 us -> 0 us
  Pallas kernels: 0 us -> 7.2 us
    all_gather x1 -> x0, waiting for transfers between devices: 109 us -> none  [on_device(): lax.all_gather(t_cycle, 'pair', axis=1, tiled=True)]
    reduce_scatter x1 -> x0, waiting for transfers between devices: 57.8 us -> none  [reduce_rows(): lax.psum_scatter(partial_value, 'ph', scatter_dimension=1, tiled=True)]
    ppermute x0 -> x5, waiting for transfers between devices: none -> 27.8 us  [shift_y(): lax.ppermute(value, AXES, list(zip(ids.ravel().tolist(), targets.ravel()....]
    all_to_all x0 -> x2, waiting for transfers between devices: none -> 23.2 us  [the longest x1 23.2 us: on_device(): lax.all_to_all(partial.reshape(NX * NZ * NC, 32, SLOTS), ('x', 'z', 'c'),...]
    all_to_all x0 -> x2, starting transfers between devices: none -> 19.6 us  [the longest x1 15.1 us: on_device(): lax.all_to_all(partial.reshape(NX * NZ * NC, 32, SLOTS), ('x', 'z', 'c'),...]
    all_to_all x0 -> x1, blocking collectives: none -> 16.6 us  [on_device(): own = lax.all_to_all(t_cycle, ('x', 'c'), 0, 0, tiled=True)]
    ppermute x0 -> x5, starting transfers between devices: none -> 13.6 us  [shift_y(): lax.ppermute(value, AXES, list(zip(ids.ravel().tolist(), targets.ravel()....]
    dot_general x2 -> x0, matrix products: 12.8 us -> none  [the longest x1 12.4 us: on_device(): jnp.einsum('grk,gkc->grc', lax.all_gather(t_cycle, 'pair', axis=1, tiled=...]
  transfers between devices with their start and end apart: 2 -> 7, of which waited for: 2 -> 6; matrix products, arithmetic and copies ran while one was open for 1% -> 5% of each run, Pallas kernels for 0% -> 0%
where the time goes in v1:
time: 117 us
  waiting for transfers between devices  51 us (44%)
  starting transfers between devices  33.2 us (28%)
  blocking collectives  16.6 us (14%)
  Pallas kernels  7.2 us (6%)
  local copies, waits for them, and re-layouts  4.58 us (4%)
  other arithmetic  3.98 us (3%)
    ppermute x5, waiting for transfers between devices, shift_y(): lax.ppermute(value, AXES, list(zip(ids.ravel().tolist(), targets.ravel()....  27.8 us
    all_to_all x1, waiting for transfers between devices, on_device(): lax.all_to_all(partial.reshape(NX * NZ * NC, 32, SLOTS), ('x', 'z', 'c'),...  23.2 us
    all_to_all x1, blocking collectives, on_device(): own = lax.all_to_all(t_cycle, ('x', 'c'), 0, 0, tiled=True)  16.6 us
    all_to_all x1, starting transfers between devices, on_device(): lax.all_to_all(partial.reshape(NX * NZ * NC, 32, SLOTS), ('x', 'z', 'c'),...  15.1 us
    ppermute x5, starting transfers between devices, shift_y(): lax.ppermute(value, AXES, list(zip(ids.ravel().tolist(), targets.ravel()....  13.6 us
    pallas_call x1, Pallas kernels, product(): pl.pallas_call(product_body, grid=(2,), in_specs=[pl.BlockSpec(memory_spa...  5.26 us
    all_to_all x1, starting transfers between devices, on_device(): w = lax.all_to_all(w_cycle, ('x', 'c'), 0, 0, tiled=True)  4.55 us
    unnamed x22, local copies, waits for them, and re-layouts  3.15 us
  transfers between devices with their start and end apart: 7, of which 6 were waited for; matrix products, arithmetic and copies ran while one was open for 5% of the time, Pallas kernels for 0%

profile of v1, /device:TPU:1, one launch (start us, length us, event | category | flops | bytes accessed | tf_op | source)
XLA Modules:
  0.0 116.8 jit_solution(17893460450059689968)
XLA Ops:
  0.0 16.6 %all_to_all.15.t0 = f32[8,16,512]{2,1,0:T(8,128)S(1)} all-to-all(f32[8,16,512]{2,1,0:T(8,128)} %param.6), channel_id=1, replica_groups=mesh['x'=4,'y'=8,'z'=8,'c'=2] {'x','c'}, dimensions={0} | all-to-all | bytes 524288 | tf_op jit(solution)/shard_map/all_to_all | solution.py:133
  16.6 0.0 copy-start.5
  16.6 4.5 %all-to-all-start.1 = ((f32[8,512,128]{2,1,0:T(8,128)}), f32[8,512,128]{2,1,0:T(8,128)S(1)}, u32[]{:S(2)}, u32[]{:S(2)}) async-start(f32[8,512,128]{2,1,0:T(8,128)} %param.7), calls=%async_computation.1 | async-start | bytes 4194304 | tf_op jit(solution)/shard_map/all_to_all | solution.py:138
  21.2 1.9 %collective-permute-start = (f32[8,16,512]{2,1,0:T(8,128)S(1)}, f32[8,16,512]{2,1,0:T(8,128)S(1)}, u32[]{:S(2)}, u32[]{:S(2)}) collective-permute-start(f32[8,16,512]{2,1,0:T(8,128)S(1)} %all_to_all.15.t0), channel_id=1, source_target_pairs={{0,112},{1,113},{2,114},{3,115},{4,116},{5,117},{6,118},{7,119},{8... | collective-permute-start | bytes 786440 | tf_op jit(solution)/shard_map/ppermute | solution.py:20
  23.1 3.4 %collective-permute-start.1 = (f32[8,16,512]{2,1,0:T(8,128)S(1)}, f32[8,16,512]{2,1,0:T(8,128)S(1)}, u32[]{:S(2)}, u32[]{:S(2)}) collective-permute-start(f32[8,16,512]{2,1,0:T(8,128)S(1)} %all_to_all.15.t0), channel_id=1, source_target_pairs={{0,16},{1,17},{2,18},{3,19},{4,20},{5,21},{6,22},{7,23},{8,24},{9,... | collective-permute-start | bytes 786440 | tf_op jit(solution)/shard_map/ppermute | solution.py:20
  26.5 0.0 copy-done.5
  26.5 3.1 %collective-permute-start.2 = (f32[8,16,512]{2,1,0:T(8,128)S(1)}, f32[8,16,512]{2,1,0:T(8,128)S(1)}, u32[]{:S(2)}, u32[]{:S(2)}) collective-permute-start(f32[8,16,512]{2,1,0:T(8,128)S(1)} %all_to_all.15.t0), channel_id=1, source_target_pairs={{0,64},{1,65},{2,66},{3,67},{4,68},{5,69},{6,70},{7,71},{8,72},{9,... | collective-permute-start | bytes 786440 | tf_op jit(solution)/shard_map/ppermute | solution.py:20
  29.6 1.2 %collective-permute-done.t1 = f32[8,16,512]{2,1,0:T(8,128)S(1)} collective-permute-done((f32[8,16,512]{2,1,0:T(8,128)S(1)}, f32[8,16,512]{2,1,0:T(8,128)S(1)}, u32[]{:S(2)}, u32[]{:S(2)}) %collective-permute-start) | collective-permute-done | bytes 262176 | tf_op jit(solution)/shard_map/ppermute | solution.py:20
  30.8 0.0 copy-start.2
  30.8 8.8 %collective-permute-done.1.t2 = f32[8,16,512]{2,1,0:T(8,128)S(1)} collective-permute-done((f32[8,16,512]{2,1,0:T(8,128)S(1)}, f32[8,16,512]{2,1,0:T(8,128)S(1)}, u32[]{:S(2)}, u32[]{:S(2)}) %collective-permute-start.1) | collective-permute-done | bytes 262176 | tf_op jit(solution)/shard_map/ppermute | solution.py:20
  39.6 0.0 copy-start.3
  39.6 6.0 %collective-permute-done.2.t3 = f32[8,16,512]{2,1,0:T(8,128)S(1)} collective-permute-done((f32[8,16,512]{2,1,0:T(8,128)S(1)}, f32[8,16,512]{2,1,0:T(8,128)S(1)}, u32[]{:S(2)}, u32[]{:S(2)}) %collective-permute-start.2) | collective-permute-done | bytes 262176 | tf_op jit(solution)/shard_map/ppermute | solution.py:20
  45.6 0.0 copy-start.4
  45.6 0.1 pad_maximum_fusion
  45.8 2.8 %collective-permute-start.3 = (f32[16,16,512]{2,1,0:T(8,128)S(1)}, f32[16,16,512]{2,1,0:T(8,128)S(1)}, u32[]{:S(2)}, u32[]{:S(2)}) collective-permute-start(f32[16,16,512]{2,1,0:T(8,128)S(1)} %get-tuple-element.14), channel_id=1, source_target_pairs={{0,112},{1,113},{2,114},{3,115},{4,116},{5,117},{6,118},{7,119},{8... | collective-permute-start | bytes 1572872 | tf_op jit(solution)/shard_map/ppermute | solution.py:20
  48.5 2.5 %collective-permute-start.4 = (f32[16,16,512]{2,1,0:T(8,128)S(1)}, f32[16,16,512]{2,1,0:T(8,128)}, u32[]{:S(2)}, u32[]{:S(2)}) collective-permute-start(f32[16,16,512]{2,1,0:T(8,128)S(1)} %get-tuple-element.13), channel_id=1, source_target_pairs={{0,16},{1,17},{2,18},{3,19},{4,20},{5,21},{6,22},{7,23},{8,24},{9,... | collective-permute-start | bytes 1572872 | tf_op jit(solution)/shard_map/ppermute | solution.py:20
  51.1 9.7 %collective-permute-done.3.t45 = f32[16,16,512]{2,1,0:T(8,128)S(1)} collective-permute-done((f32[16,16,512]{2,1,0:T(8,128)S(1)}, f32[16,16,512]{2,1,0:T(8,128)S(1)}, u32[]{:S(2)}, u32[]{:S(2)}) %collective-permute-start.3) | collective-permute-done | bytes 524320 | tf_op jit(solution)/shard_map/ppermute | solution.py:20
  60.7 0.0 copy-start.6
  60.7 0.8 copy-done.6
  61.5 2.1 %collective-permute-done.4.t67 = f32[16,16,512]{2,1,0:T(8,128)} collective-permute-done((f32[16,16,512]{2,1,0:T(8,128)S(1)}, f32[16,16,512]{2,1,0:T(8,128)}, u32[]{:S(2)}, u32[]{:S(2)}) %collective-permute-start.4) | collective-permute-done | bytes 524320 | tf_op jit(solution)/shard_map/ppermute | solution.py:20
  63.7 0.0 all-to-all-done.1.w_ref
  63.7 0.0 copy-done.2
  63.7 0.0 copy-done.3
  63.7 0.0 copy-done.4
  63.7 0.0 copy-start
  63.7 1.3 %copy-done = f32[8,512,128]{2,1,0:T(8,128)} copy-done((f32[8,512,128]{2,1,0:T(8,128)}, f32[8,512,128]{2,1,0:T(8,128)S(1)}, u32[]{:S(2)}) %copy-start) | copy-done | bytes 2097176
  65.0 5.3 %product.1 = f32[4,4,128,128]{3,2,1,0:T(8,128)} custom-call(s32[64]{0:T(128)} %occ_ref.1, s32[8]{0:T(128)} %count_ref.1, f32[8,16,512]{2,1,0:T(8,128)} %copy-done.5, f32[8,16,512]{2,1,0:T(8,128)} %copy-done.2, f32[8,16,512]{2,1,0:T(8,128)} %copy-done.3, f32[8,16,512]{2,1,0:T(8,128)} %copy-done.4, f32[16,16,512]{2,1,0:T(8,128)} %copy-done.6, ...), custom_call_target="tpu_custom_call" | custom-call | tf_op jit(solution)/shard_map/product/pallas_call | solution.py:72
  70.3 0.0 copy-start.7
  70.3 0.0 copy-start.10
  70.3 0.0 copy-start.8
  70.3 0.0 copy-start.9
  70.3 15.1 %all-to-all-start.2 = ((f32[64,32,128]{2,1,0:T(8,128)}), f32[64,32,128]{2,1,0:T(8,128)S(1)}, u32[]{:S(2)}, u32[]{:S(2)}) async-start(f32[64,32,128]{2,1,0:T(8,128)} %bitcast.7), calls=%async_computation.2 | async-start | bytes 2097152 | tf_op jit(solution)/shard_map/all_to_all | solution.py:143
  85.4 0.0 copy-done.7
  85.4 0.6 fusion.3
  86.0 0.0 copy-done.10
  86.0 0.6 fusion.2
  86.7 0.6 iota_xor_fusion
  87.3 0.6 iota_xor_fusion.1
  88.0 0.1 iota_compare_fusion
  88.1 0.0 copy-done.8
  88.1 0.1 select_reduce_fusion.1
  88.2 0.6 broadcast_subtract_fusion.1
  88.8 0.1 constant_dynamic-slice_fusion.1
  88.9 0.0 copy-done.9
  88.9 0.2 select_reduce_fusion.3
  89.1 0.1 fusion
  89.2 0.1 constant_dynamic-slice_fusion
  89.2 0.1 fusion.1
  89.3 0.6 broadcast_subtract_fusion
  90.0 0.8 add_divide_fusion.factor_ref
  90.7 23.2 %all-to-all-done.2 = f32[64,32,128]{2,1,0:T(8,128)S(1)} async-done(((f32[64,32,128]{2,1,0:T(8,128)}), f32[64,32,128]{2,1,0:T(8,128)S(1)}, u32[]{:S(2)}, u32[]{:S(2)}) %all-to-all-start.2) | async-done | bytes 1048608 | tf_op jit(solution)/shard_map/all_to_all | solution.py:143
  113.9 0.0 copy-start.1
  113.9 1.0 copy-done.1
  114.9 1.9 %finish.1 = f32[8,32,128]{2,1,0:T(8,128)} custom-call(f32[4,8,2,32,128]{4,3,2,1,0:T(8,128)} %bitcast.6, f32[8,32,128]{2,1,0:T(8,128)} %add_divide_fusion.factor_ref), custom_call_target="tpu_custom_call" | custom-call | tf_op jit(solution)/shard_map/finish/pallas_call | solution.py:103
Async XLA Ops:
  16.6 9.8 %copy-start.5 = (f32[8,16,512]{2,1,0:T(8,128)}, f32[8,16,512]{2,1,0:T(8,128)S(1)}, u32[]{:S(2)}) copy-start(f32[8,16,512]{2,1,0:T(8,128)S(1)} %all_to_all.15.t0) | copy-start | bytes 786436
  16.6 47.0 %all-to-all-start.1 = ((f32[8,512,128]{2,1,0:T(8,128)}), f32[8,512,128]{2,1,0:T(8,128)S(1)}, u32[]{:S(2)}, u32[]{:S(2)}) async-start(f32[8,512,128]{2,1,0:T(8,128)} %param.7), calls=%async_computation.1 | async-start | bytes 4194304 | tf_op jit(solution)/shard_map/all_to_all | solution.py:138
  21.2 9.6 %collective-permute-start = (f32[8,16,512]{2,1,0:T(8,128)S(1)}, f32[8,16,512]{2,1,0:T(8,128)S(1)}, u32[]{:S(2)}, u32[]{:S(2)}) collective-permute-start(f32[8,16,512]{2,1,0:T(8,128)S(1)} %all_to_all.15.t0), channel_id=1, source_target_pairs={{0,112},{1,113},{2,114},{3,115},{4,116},{5,117},{6,118},{7,119},{8... | collective-permute-start | bytes 786440 | tf_op jit(solution)/shard_map/ppermute | solution.py:20
  23.1 16.5 %collective-permute-start.1 = (f32[8,16,512]{2,1,0:T(8,128)S(1)}, f32[8,16,512]{2,1,0:T(8,128)S(1)}, u32[]{:S(2)}, u32[]{:S(2)}) collective-permute-start(f32[8,16,512]{2,1,0:T(8,128)S(1)} %all_to_all.15.t0), channel_id=1, source_target_pairs={{0,16},{1,17},{2,18},{3,19},{4,20},{5,21},{6,22},{7,23},{8,24},{9,... | collective-permute-start | bytes 786440 | tf_op jit(solution)/shard_map/ppermute | solution.py:20
  26.5 19.2 %collective-permute-start.2 = (f32[8,16,512]{2,1,0:T(8,128)S(1)}, f32[8,16,512]{2,1,0:T(8,128)S(1)}, u32[]{:S(2)}, u32[]{:S(2)}) collective-permute-start(f32[8,16,512]{2,1,0:T(8,128)S(1)} %all_to_all.15.t0), channel_id=1, source_target_pairs={{0,64},{1,65},{2,66},{3,67},{4,68},{5,69},{6,70},{7,71},{8,72},{9,... | collective-permute-start | bytes 786440 | tf_op jit(solution)/shard_map/ppermute | solution.py:20
  30.8 32.9 %copy-start.2 = (f32[8,16,512]{2,1,0:T(8,128)}, f32[8,16,512]{2,1,0:T(8,128)S(1)}, u32[]{:S(2)}) copy-start(f32[8,16,512]{2,1,0:T(8,128)S(1)} %collective-permute-done.t1) | copy-start | bytes 786436
  39.6 24.0 %copy-start.3 = (f32[8,16,512]{2,1,0:T(8,128)}, f32[8,16,512]{2,1,0:T(8,128)S(1)}, u32[]{:S(2)}) copy-start(f32[8,16,512]{2,1,0:T(8,128)S(1)} %collective-permute-done.1.t2) | copy-start | bytes 786436
  45.6 18.0 %copy-start.4 = (f32[8,16,512]{2,1,0:T(8,128)}, f32[8,16,512]{2,1,0:T(8,128)S(1)}, u32[]{:S(2)}) copy-start(f32[8,16,512]{2,1,0:T(8,128)S(1)} %collective-permute-done.2.t3) | copy-start | bytes 786436
  45.8 15.0 %collective-permute-start.3 = (f32[16,16,512]{2,1,0:T(8,128)S(1)}, f32[16,16,512]{2,1,0:T(8,128)S(1)}, u32[]{:S(2)}, u32[]{:S(2)}) collective-permute-start(f32[16,16,512]{2,1,0:T(8,128)S(1)} %get-tuple-element.14), channel_id=1, source_target_pairs={{0,112},{1,113},{2,114},{3,115},{4,116},{5,117},{6,118},{7,119},{8... | collective-permute-start | bytes 1572872 | tf_op jit(solution)/shard_map/ppermute | solution.py:20
  48.5 15.1 %collective-permute-start.4 = (f32[16,16,512]{2,1,0:T(8,128)S(1)}, f32[16,16,512]{2,1,0:T(8,128)}, u32[]{:S(2)}, u32[]{:S(2)}) collective-permute-start(f32[16,16,512]{2,1,0:T(8,128)S(1)} %get-tuple-element.13), channel_id=1, source_target_pairs={{0,16},{1,17},{2,18},{3,19},{4,20},{5,21},{6,22},{7,23},{8,24},{9,... | collective-permute-start | bytes 1572872 | tf_op jit(solution)/shard_map/ppermute | solution.py:20
  60.7 0.8 copy-start.6
  63.7 1.3 %copy-start = (f32[8,512,128]{2,1,0:T(8,128)}, f32[8,512,128]{2,1,0:T(8,128)S(1)}, u32[]{:S(2)}) copy-start(f32[8,512,128]{2,1,0:T(8,128)S(1)} %all-to-all-done.1.w_ref) | copy-start | bytes 6291460
  70.3 15.1 %copy-start.7 = (s32[64]{0:T(128)S(1)}, s32[64]{0:T(128)}, u32[]{:S(2)}) copy-start(s32[64]{0:T(128)} %occ_ref.1) | copy-start | bytes 772
  70.3 15.8 %copy-start.10 = (f32[64]{0:T(128)S(1)}, f32[64]{0:T(128)}, u32[]{:S(2)}) copy-start(f32[64]{0:T(128)} %param.8) | copy-start | bytes 772
  70.3 17.8 %copy-start.8 = (f32[8,128]{1,0:T(8,128)S(1)}, f32[8,128]{1,0:T(8,128)}, u32[]{:S(2)}) copy-start(f32[8,128]{1,0:T(8,128)} %param.9) | copy-start | bytes 12292
  70.3 18.6 %copy-start.9 = (s32[8]{0:T(128)S(1)}, s32[8]{0:T(128)}, u32[]{:S(2)}) copy-start(s32[8]{0:T(128)} %count_ref.1) | copy-start | bytes 100
  70.3 43.6 %all-to-all-start.2 = ((f32[64,32,128]{2,1,0:T(8,128)}), f32[64,32,128]{2,1,0:T(8,128)S(1)}, u32[]{:S(2)}, u32[]{:S(2)}) async-start(f32[64,32,128]{2,1,0:T(8,128)} %bitcast.7), calls=%async_computation.2 | async-start | bytes 2097152 | tf_op jit(solution)/shard_map/all_to_all | solution.py:143
  113.9 1.0 copy-start.1

commit v2 on v1

v2 whole, which is shorter than its diff:
```python
import functools

import jax
import jax.numpy as jnp
import numpy as np
from jax import lax
from jax.experimental import pallas as pl
from jax.experimental.pallas import tpu as pltpu
from jax.sharding import Mesh, PartitionSpec as P

IRREPS = 8
SLOTS = 128
NX, NY, NZ, NC = 4, 8, 8, 2
AXES = ("x", "y", "z", "c")
K_LOCAL = 512
OFFSETS = (0, 2, 6, 4)


IDS = np.arange(NX * NY * NZ * NC).reshape(NX, NY, NZ, NC)


def send(value, axis, first, second):
    targets = np.stack([np.roll(IDS[..., 0], -first, axis=axis), np.roll(IDS[..., 1], -second, axis=axis)], axis=-1)
    return lax.ppermute(value, AXES, list(zip(IDS.ravel().tolist(), targets.ravel().tolist())))


def split(value):
    high = value.astype(jnp.bfloat16)
    low = (value - high.astype(jnp.float32)).astype(jnp.bfloat16)
    return high, low


def product_body(first_half, occ_ref, count_ref, *refs):
    *t_refs, w_ref, same_ref, other_ref, t_high, t_low, w_high, w_low = refs
    y = lax.axis_index("y")
    z = lax.axis_index("z")
    c_own = lax.axis_index("c")
    g = lax.axis_index("x") * NC + c_own
    base = y if first_half else y + 1 + 6 * c_own

    for slot in range(4):
        ref, first = (t_refs[slot], 0) if first_half else (t_refs[0], slot * 8)
        for i in range(NX):
            for c in range(NC):
                high, low = split(ref[first + i * NC + c])
                rows = pl.ds((slot * NX + i) * 16, 16)
                cols = pl.ds(c * K_LOCAL, K_LOCAL)
                t_high[rows, cols] = high
                t_low[rows, cols] = low

    slots = lax.broadcasted_iota(jnp.int32, (SLOTS, SLOTS), 0)
    for c in range(NC):
        for k in range(4):
            live = slots < count_ref[jnp.bitwise_xor(occ_ref[z * 8 + c * 4 + k], g)]
            for col in range(NX):
                part = jnp.where(live, w_ref[col * NC + c, pl.ds(k * SLOTS, SLOTS), :], 0.0)
                high, low = split(part)
                rows = pl.ds(c * K_LOCAL + k * SLOTS, SLOTS)
                cols = pl.ds(col * SLOTS, SLOTS)
                w_high[rows, cols] = high
                w_low[rows, cols] = low

    def dot(a, b):
        return jnp.dot(a[...], b[...], preferred_element_type=jnp.float32)

    total = dot(t_high, w_low) + dot(t_low, w_high) + dot(t_high, w_high)
    for slot, offset in enumerate(OFFSETS):
        quarter = lax.rem(base + offset, NY) // 2
        for i in range(NX):
            for col in range(NX):
                rows = slice((slot * NX + i) * 16, (slot * NX + i + 1) * 16)
                value = total[rows, col * SLOTS : (col + 1) * SLOTS]
                if first_half:
                    same_ref[col, i * 4 + quarter] = value
                else:
                    spot = i * NC + lax.rem(quarter, 2)
                    mine = lax.rem(quarter // 2 + z, 2) == 0

                    @pl.when(mine)
                    def _():
                        same_ref[col, spot] = value

                    @pl.when(jnp.logical_not(mine))
                    def _():
                        other_ref[col, spot] = value


def product(first_half, occ_irrep, vir_count, blocks, w):
    shape = jax.ShapeDtypeStruct((NX, 16 if first_half else 8, 16, SLOTS), jnp.float32)
    body = functools.partial(product_body, first_half)
    if first_half:
        body = lambda *refs: product_body(True, *refs[:8], None, *refs[8:])
    return pl.pallas_call(
        body,
        in_specs=[pl.BlockSpec(memory_space=pltpu.SMEM)] * 2
        + [pl.BlockSpec(memory_space=pltpu.VMEM)] * (len(blocks) + 1),
        out_shape=shape if first_half else (shape, shape),
        scratch_shapes=[
            pltpu.VMEM((256, 2 * K_LOCAL), jnp.bfloat16),
            pltpu.VMEM((256, 2 * K_LOCAL), jnp.bfloat16),
            pltpu.VMEM((2 * K_LOCAL, NX * SLOTS), jnp.bfloat16),
            pltpu.VMEM((2 * K_LOCAL, NX * SLOTS), jnp.bfloat16),
        ],
        name="first_product" if first_half else "second_product",
    )(occ_irrep, vir_count, *blocks, w)


def finish_body(first_ref, second_ref, factor_ref, out_ref):
    parity = lax.rem(lax.axis_index("y"), 2)
    for ref, part in ((first_ref, parity), (second_ref, 1 - parity)):
        rows = pl.ds(pl.multiple_of(part * 16, 16), 16)
        for x in range(NX):
            for c in range(NC):
                total = ref[x, 0, c]
                for z in range(1, ref.shape[1]):
                    total = total + ref[x, z, c]
                out_ref[x * NC + c, rows, :] = total * factor_ref[x * NC + c, rows, :]


def finish(first, second, factor):
    return pl.pallas_call(
        finish_body,
        out_shape=jax.ShapeDtypeStruct((IRREPS, 32, SLOTS), jnp.float32),
        name="finish",
    )(first, second, factor)


def factors(occ_energy, vir_energy, occ_irrep, vir_count):
    row_i = lax.axis_index("z") // 2
    row_a = (lax.axis_index("z") % 2 * NC + lax.axis_index("c")) * 32
    col_j = lax.axis_index("x") * NY + lax.axis_index("y")
    irreps = jnp.arange(IRREPS, dtype=jnp.int32)
    slots = jnp.arange(SLOTS, dtype=jnp.int32)

    def side(occupied):
        label = jnp.bitwise_xor(lax.dynamic_index_in_dim(occ_irrep, occupied, 0, False), irreps)
        onehot = label[:, None] == irreps[None, :]
        count = jnp.sum(jnp.where(onehot, vir_count[None, :], 0), axis=1)
        energy = jnp.sum(jnp.where(onehot[:, :, None], vir_energy[None], 0.0), axis=1)
        energy = lax.dynamic_index_in_dim(occ_energy, occupied, 0, False) - energy
        return energy, (slots[None, :] < count[:, None]).astype(jnp.float32)

    e_row, m_row = side(row_i)
    e_col, m_col = side(col_j)
    e_row = lax.dynamic_slice_in_dim(e_row, row_a, 32, 1)
    m_row = lax.dynamic_slice_in_dim(m_row, row_a, 32, 1)
    return m_row[:, :, None] * m_col[:, None, :] / (e_row[:, :, None] + e_col[:, None, :])


def on_device(t_cycle, w_cycle, occ_energy, vir_energy, occ_irrep, vir_count):
    own = lax.all_to_all(t_cycle, ("x", "c"), 0, 0, tiled=True)
    w_cycle, own = lax.optimization_barrier((w_cycle, own))
    w = lax.all_to_all(w_cycle, ("x", "c"), 0, 0, tiled=True)
    blocks = (own, send(own, 1, -2, -2), send(own, 1, 2, 2), send(own, 1, 4, 4))
    others = send(jnp.concatenate(blocks, axis=0), 1, -1, 1)
    first = product(True, occ_irrep, vir_count, blocks, w)
    first = lax.all_to_all(first.reshape(NX * NZ * NC, 16, SLOTS), ("x", "z", "c"), 0, 0, tiled=True)
    same, other = product(False, occ_irrep, vir_count, (others,), w)
    arrived = send(other, 2, 1, -1)
    second = same + arrived
    peers = np.moveaxis(IDS.reshape(NX, NY, NZ // 2, 2, NC), (1, 3), (0, 1)).reshape(NY * 2, -1)
    second = lax.all_to_all(
        second.reshape(NX * NZ // 2 * NC, 16, SLOTS), AXES, 0, 0, tiled=True, axis_index_groups=peers.tolist()
    )
    factor = factors(occ_energy, vir_energy, occ_irrep, vir_count)
    return finish(first.reshape(NX, NZ, NC, 16, SLOTS), second.reshape(NX, NZ // 2, NC, 16, SLOTS), factor)


def solution(mesh):
    grid = Mesh(mesh.devices.reshape(NX, NY, NZ, NC), AXES)
    return jax.shard_map(
        on_device,
        mesh=grid,
        in_specs=(P(None, ("x", "y"), ("z", "c")), P(None, ("z", "c"), ("x", "y")), P(), P(), P(), P()),
        out_specs=P(None, ("z", "c"), ("x", "y")),
        check_vma=False,
    )
```

time: 117 us -> 138 us (1.18)
  the two profiles are of different devices: /device:TPU:1 before, /device:TPU:23 now
where the time goes in v2:
time: 138 us
  starting transfers between devices  54.7 us (40%)
  waiting for transfers between devices  51.6 us (37%)
  Pallas kernels  10.3 us (7%)
  blocking collectives  9.85 us (7%)
  other arithmetic  5.79 us (4%)
  local copies, waits for them, and re-layouts  5.32 us (4%)
    ppermute x5, starting transfers between devices, send(): lax.ppermute(value, AXES, list(zip(IDS.ravel().tolist(), targets.ravel()....  31.2 us
    ppermute x5, waiting for transfers between devices, send(): lax.ppermute(value, AXES, list(zip(IDS.ravel().tolist(), targets.ravel()....  30.8 us
    all_to_all x1, waiting for transfers between devices, on_device(): lax.all_to_all(first.reshape(NX * NZ * NC, 16, SLOTS), ('x', 'z', 'c'), 0...  15.4 us
    all_to_all x1, starting transfers between devices, on_device(): lax.all_to_all(second.reshape(NX * NZ // 2 * NC, 16, SLOTS), AXES, 0, 0,...  10.5 us
    all_to_all x1, blocking collectives, on_device(): own = lax.all_to_all(t_cycle, ('x', 'c'), 0, 0, tiled=True)  9.85 us
    pallas_call x2, Pallas kernels, product(): pl.pallas_call(body, in_specs=[pl.BlockSpec(memory_space=pltpu.SMEM)] * 2...  8.42 us
    all_to_all x1, starting transfers between devices, on_device(): lax.all_to_all(first.reshape(NX * NZ * NC, 16, SLOTS), ('x', 'z', 'c'), 0...  6.83 us
    all_to_all x1, starting transfers between devices, on_device(): w = lax.all_to_all(w_cycle, ('x', 'c'), 0, 0, tiled=True)  6.26 us
  transfers between devices with their start and end apart: 8, of which 7 were waited for; matrix products, arithmetic and copies ran while one was open for 4% of the time, Pallas kernels for 3%

profile of v2, /device:TPU:23, one launch (start us, length us, event | category | flops | bytes accessed | tf_op | source)
XLA Modules:
  0.0 137.7 jit_solution(2417300353042362638)
XLA Ops:
  0.0 9.8 %all_to_all.20.refs_2_ = f32[8,16,512]{2,1,0:T(8,128)S(1)} all-to-all(f32[8,16,512]{2,1,0:T(8,128)} %param.6), channel_id=1, replica_groups=mesh['x'=4,'y'=8,'z'=8,'c'=2] {'x','c'}, dimensions={0} | all-to-all | bytes 524288 | tf_op jit(solution)/shard_map/all_to_all | solution.py:151
  9.8 0.0 copy-start.1
  9.8 6.3 %all-to-all-start.1 = ((f32[8,512,128]{2,1,0:T(8,128)}), f32[8,512,128]{2,1,0:T(8,128)S(1)}, u32[]{:S(2)}, u32[]{:S(2)}) async-start(f32[8,512,128]{2,1,0:T(8,128)} %param.7), calls=%async_computation.1 | async-start | bytes 4194304 | tf_op jit(solution)/shard_map/all_to_all | solution.py:153
  16.1 6.3 %collective-permute-start = (f32[8,16,512]{2,1,0:T(8,128)S(1)}, f32[8,16,512]{2,1,0:T(8,128)S(1)}, u32[]{:S(2)}, u32[]{:S(2)}) collective-permute-start(f32[8,16,512]{2,1,0:T(8,128)S(1)} %all_to_all.20.refs_2_), channel_id=1, source_target_pairs={{0,96},{1,97},{2,98},{3,99},{4,100},{5,101},{6,102},{7,103},{8,104... | collective-permute-start | bytes 786440 | tf_op jit(solution)/shard_map/ppermute | solution.py:24
  22.4 1.9 %collective-permute-start.1 = (f32[8,16,512]{2,1,0:T(8,128)S(1)}, f32[8,16,512]{2,1,0:T(8,128)S(1)}, u32[]{:S(2)}, u32[]{:S(2)}) collective-permute-start(f32[8,16,512]{2,1,0:T(8,128)S(1)} %all_to_all.20.refs_2_), channel_id=1, source_target_pairs={{0,32},{1,33},{2,34},{3,35},{4,36},{5,37},{6,38},{7,39},{8,40},{9,... | collective-permute-start | bytes 786440 | tf_op jit(solution)/shard_map/ppermute | solution.py:24
  24.4 5.2 %collective-permute-start.2 = (f32[8,16,512]{2,1,0:T(8,128)S(1)}, f32[8,16,512]{2,1,0:T(8,128)S(1)}, u32[]{:S(2)}, u32[]{:S(2)}) collective-permute-start(f32[8,16,512]{2,1,0:T(8,128)S(1)} %all_to_all.20.refs_2_), channel_id=1, source_target_pairs={{0,64},{1,65},{2,66},{3,67},{4,68},{5,69},{6,70},{7,71},{8,72},{9,... | collective-permute-start | bytes 786440 | tf_op jit(solution)/shard_map/ppermute | solution.py:24
  29.6 4.2 %collective-permute-done.refs_3_ = f32[8,16,512]{2,1,0:T(8,128)S(1)} collective-permute-done((f32[8,16,512]{2,1,0:T(8,128)S(1)}, f32[8,16,512]{2,1,0:T(8,128)S(1)}, u32[]{:S(2)}, u32[]{:S(2)}) %collective-permute-start) | collective-permute-done | bytes 262176 | tf_op jit(solution)/shard_map/ppermute | solution.py:24
  33.8 0.0 copy-start.5
  33.8 5.1 %collective-permute-done.1.refs_4_ = f32[8,16,512]{2,1,0:T(8,128)S(1)} collective-permute-done((f32[8,16,512]{2,1,0:T(8,128)S(1)}, f32[8,16,512]{2,1,0:T(8,128)S(1)}, u32[]{:S(2)}, u32[]{:S(2)}) %collective-permute-start.1) | collective-permute-done | bytes 262176 | tf_op jit(solution)/shard_map/ppermute | solution.py:24
  38.9 0.0 copy-start.6
  38.9 8.1 %collective-permute-done.2.refs_5_ = f32[8,16,512]{2,1,0:T(8,128)S(1)} collective-permute-done((f32[8,16,512]{2,1,0:T(8,128)S(1)}, f32[8,16,512]{2,1,0:T(8,128)S(1)}, u32[]{:S(2)}, u32[]{:S(2)}) %collective-permute-start.2) | collective-permute-done | bytes 262176 | tf_op jit(solution)/shard_map/ppermute | solution.py:24
  47.0 0.0 copy-done.1
  47.0 0.0 copy-done.6
  47.0 0.0 copy-start.7
  47.0 0.7 copy-done.7
  47.7 0.1 pad_maximum_fusion
  47.8 0.0 copy-start.8
  47.8 0.0 copy-start.11
  47.8 0.0 copy-start.9
  47.8 0.0 copy-start.10
  47.8 4.1 %collective-permute-start.3 = (f32[32,16,512]{2,1,0:T(8,128)S(1)}, f32[32,16,512]{2,1,0:T(8,128)S(1)}, u32[]{:S(2)}, u32[]{:S(2)}) collective-permute-start(f32[32,16,512]{2,1,0:T(8,128)S(1)} %pad_maximum_fusion), channel_id=1, source_target_pairs={{0,112},{1,17},{2,114},{3,19},{4,116},{5,21},{6,118},{7,23},{8,120... | collective-permute-start | bytes 3145736 | tf_op jit(solution)/shard_map/ppermute | solution.py:24
  51.9 11.8 %collective-permute-done.3.refs_0_ = f32[32,16,512]{2,1,0:T(8,128)S(1)} collective-permute-done((f32[32,16,512]{2,1,0:T(8,128)S(1)}, f32[32,16,512]{2,1,0:T(8,128)S(1)}, u32[]{:S(2)}, u32[]{:S(2)}) %collective-permute-start.3) | collective-permute-done | bytes 1048608 | tf_op jit(solution)/shard_map/ppermute | solution.py:24
  63.8 0.0 copy-start.3
  63.8 0.0 all-to-all-done.1.refs_6_.refs_1_
  63.8 1.0 copy-done.3
  64.7 0.0 copy-start
  64.7 1.3 copy-done
  66.1 4.4 %second_product.1 = (f32[4,8,16,128]{3,2,1,0:T(8,128)}, f32[4,8,16,128]{3,2,1,0:T(8,128)}) custom-call(s32[64]{0:T(128)} %occ_ref.1, s32[8]{0:T(128)} %count_ref.1, f32[32,16,512]{2,1,0:T(8,128)} %copy-done.3, f32[8,512,128]{2,1,0:T(8,128)} %copy-done), custom_call_target="tpu_custom_call" | custom-call | tf_op jit(solution)/shard_map/second_product/pallas_call | solution.py:93
  70.5 0.0 copy-done.5
  70.5 13.6 %collective-permute-start.4 = (f32[4,8,16,128]{3,2,1,0:T(8,128)}, f32[4,8,16,128]{3,2,1,0:T(8,128)S(1)}, u32[]{:S(2)}, u32[]{:S(2)}) collective-permute-start(f32[4,8,16,128]{3,2,1,0:T(8,128)} %get-tuple-element.12), channel_id=1, source_target_pairs={{0,2},{1,15},{2,4},{3,1},{4,6},{5,3},{6,8},{7,5},{8,10},{9,7},{10,... | collective-permute-start | bytes 786440 | tf_op jit(solution)/shard_map/ppermute | solution.py:24
  84.1 0.0 copy-done.8
  84.1 0.7 fusion.3
  84.8 0.6 iota_xor_fusion
  85.5 0.7 iota_xor_fusion.1
  86.2 1.6 %collective-permute-done.4 = f32[4,8,16,128]{3,2,1,0:T(8,128)S(1)} collective-permute-done((f32[4,8,16,128]{3,2,1,0:T(8,128)}, f32[4,8,16,128]{3,2,1,0:T(8,128)S(1)}, u32[]{:S(2)}, u32[]{:S(2)}) %collective-permute-start.4) | collective-permute-done | bytes 262176 | tf_op jit(solution)/shard_map/ppermute | solution.py:24
  87.7 1.7 %add.41 = f32[4,8,16,128]{3,2,1,0:T(8,128)} add(f32[4,8,16,128]{3,2,1,0:T(8,128)} %get-tuple-element.11, f32[4,8,16,128]{3,2,1,0:T(8,128)S(1)} %collective-permute-done.4) | non-fusion elementwise | flops 65536 | bytes 786432 | tf_op jit(solution)/shard_map/add | solution.py:160
  89.4 10.5 %all-to-all-start.3 = ((f32[32,16,128]{2,1,0:T(8,128)}), f32[32,16,128]{2,1,0:T(8,128)S(1)}, u32[]{:S(2)}, u32[]{:S(2)}) async-start(f32[32,16,128]{2,1,0:T(8,128)} %bitcast.2), calls=%async_computation.3 | async-start | bytes 524288 | tf_op jit(solution)/shard_map/all_to_all | solution.py:162
  99.9 0.1 iota_compare_fusion
  100.0 0.0 copy-done.11
  100.0 0.7 fusion.2
  100.7 0.0 copy-done.9
  100.7 0.2 select_reduce_fusion.3
  100.9 0.0 copy-done.10
  100.9 0.1 select_reduce_fusion.1
  101.0 0.7 broadcast_subtract_fusion.1
  101.6 4.0 %first_product.1 = f32[4,16,16,128]{3,2,1,0:T(8,128)} custom-call(s32[64]{0:T(128)} %occ_ref.1, s32[8]{0:T(128)} %count_ref.1, f32[8,16,512]{2,1,0:T(8,128)} %copy-done.1, f32[8,16,512]{2,1,0:T(8,128)} %copy-done.5, f32[8,16,512]{2,1,0:T(8,128)} %copy-done.6, f32[8,16,512]{2,1,0:T(8,128)} %copy-done.7, f32[8,512,128]{2,1,0:T(8,128)} %copy-done), custom_call_target="tpu_custom_call" | custom-call | tf_op jit(solution)/shard_map/first_product/pallas_call | solution.py:93
  105.6 5.4 %all-to-all-done.3 = f32[32,16,128]{2,1,0:T(8,128)S(1)} async-done(((f32[32,16,128]{2,1,0:T(8,128)}), f32[32,16,128]{2,1,0:T(8,128)S(1)}, u32[]{:S(2)}, u32[]{:S(2)}) %all-to-all-start.3) | async-done | bytes 262176 | tf_op jit(solution)/shard_map/all_to_all | solution.py:162
  111.1 0.0 copy-start.4
  111.1 6.8 %all-to-all-start.2 = ((f32[64,16,128]{2,1,0:T(8,128)}), f32[64,16,128]{2,1,0:T(8,128)S(1)}, u32[]{:S(2)}, u32[]{:S(2)}) async-start(f32[64,16,128]{2,1,0:T(8,128)} %bitcast.9), calls=%async_computation.2 | async-start | bytes 1048576 | tf_op jit(solution)/shard_map/all_to_all | solution.py:157
  117.9 0.1 constant_dynamic-slice_fusion.1
  118.0 0.1 fusion
  118.1 0.1 constant_dynamic-slice_fusion
  118.1 0.1 fusion.1
  118.2 0.7 broadcast_subtract_fusion
  118.9 0.8 add_divide_fusion.factor_ref
  119.7 15.4 %all-to-all-done.2 = f32[64,16,128]{2,1,0:T(8,128)S(1)} async-done(((f32[64,16,128]{2,1,0:T(8,128)}), f32[64,16,128]{2,1,0:T(8,128)S(1)}, u32[]{:S(2)}, u32[]{:S(2)}) %all-to-all-start.2) | async-done | bytes 524320 | tf_op jit(solution)/shard_map/all_to_all | solution.py:157
  135.1 0.0 copy-start.2
  135.1 0.0 copy-done.4
  135.1 0.8 copy-done.2
  135.9 1.8 %finish.1 = f32[8,32,128]{2,1,0:T(8,128)} custom-call(f32[4,8,2,16,128]{4,3,2,1,0:T(8,128)} %bitcast.8, f32[4,4,2,16,128]{4,3,2,1,0:T(8,128)} %bitcast.10, f32[8,32,128]{2,1,0:T(8,128)} %add_divide_fusion.factor_ref), custom_call_target="tpu_custom_call" | custom-call | tf_op jit(solution)/shard_map/finish/pallas_call | solution.py:121
Async XLA Ops:
  9.8 37.1 %copy-start.1 = (f32[8,16,512]{2,1,0:T(8,128)}, f32[8,16,512]{2,1,0:T(8,128)S(1)}, u32[]{:S(2)}) copy-start(f32[8,16,512]{2,1,0:T(8,128)S(1)} %all_to_all.20.refs_2_) | copy-start | bytes 786436
  9.8 53.9 %all-to-all-start.1 = ((f32[8,512,128]{2,1,0:T(8,128)}), f32[8,512,128]{2,1,0:T(8,128)S(1)}, u32[]{:S(2)}, u32[]{:S(2)}) async-start(f32[8,512,128]{2,1,0:T(8,128)} %param.7), calls=%async_computation.1 | async-start | bytes 4194304 | tf_op jit(solution)/shard_map/all_to_all | solution.py:153
  16.1 17.6 %collective-permute-start = (f32[8,16,512]{2,1,0:T(8,128)S(1)}, f32[8,16,512]{2,1,0:T(8,128)S(1)}, u32[]{:S(2)}, u32[]{:S(2)}) collective-permute-start(f32[8,16,512]{2,1,0:T(8,128)S(1)} %all_to_all.20.refs_2_), channel_id=1, source_target_pairs={{0,96},{1,97},{2,98},{3,99},{4,100},{5,101},{6,102},{7,103},{8,104... | collective-permute-start | bytes 786440 | tf_op jit(solution)/shard_map/ppermute | solution.py:24
  22.4 16.4 %collective-permute-start.1 = (f32[8,16,512]{2,1,0:T(8,128)S(1)}, f32[8,16,512]{2,1,0:T(8,128)S(1)}, u32[]{:S(2)}, u32[]{:S(2)}) collective-permute-start(f32[8,16,512]{2,1,0:T(8,128)S(1)} %all_to_all.20.refs_2_), channel_id=1, source_target_pairs={{0,32},{1,33},{2,34},{3,35},{4,36},{5,37},{6,38},{7,39},{8,40},{9,... | collective-permute-start | bytes 786440 | tf_op jit(solution)/shard_map/ppermute | solution.py:24
  24.4 22.6 %collective-permute-start.2 = (f32[8,16,512]{2,1,0:T(8,128)S(1)}, f32[8,16,512]{2,1,0:T(8,128)S(1)}, u32[]{:S(2)}, u32[]{:S(2)}) collective-permute-start(f32[8,16,512]{2,1,0:T(8,128)S(1)} %all_to_all.20.refs_2_), channel_id=1, source_target_pairs={{0,64},{1,65},{2,66},{3,67},{4,68},{5,69},{6,70},{7,71},{8,72},{9,... | collective-permute-start | bytes 786440 | tf_op jit(solution)/shard_map/ppermute | solution.py:24
  33.8 36.7 %copy-start.5 = (f32[8,16,512]{2,1,0:T(8,128)}, f32[8,16,512]{2,1,0:T(8,128)S(1)}, u32[]{:S(2)}) copy-start(f32[8,16,512]{2,1,0:T(8,128)S(1)} %collective-permute-done.refs_3_) | copy-start | bytes 786436
  38.9 8.1 %copy-start.6 = (f32[8,16,512]{2,1,0:T(8,128)}, f32[8,16,512]{2,1,0:T(8,128)S(1)}, u32[]{:S(2)}) copy-start(f32[8,16,512]{2,1,0:T(8,128)S(1)} %collective-permute-done.1.refs_4_) | copy-start | bytes 786436
  47.0 0.7 copy-start.7
  47.8 36.4 %copy-start.8 = (s32[64]{0:T(128)S(1)}, s32[64]{0:T(128)}, u32[]{:S(2)}) copy-start(s32[64]{0:T(128)} %occ_ref.1) | copy-start | bytes 772
  47.8 52.2 %copy-start.11 = (f32[64]{0:T(128)S(1)}, f32[64]{0:T(128)}, u32[]{:S(2)}) copy-start(f32[64]{0:T(128)} %param.8) | copy-start | bytes 772
  47.8 52.9 %copy-start.9 = (s32[8]{0:T(128)S(1)}, s32[8]{0:T(128)}, u32[]{:S(2)}) copy-start(s32[8]{0:T(128)} %count_ref.1) | copy-start | bytes 100
  47.8 53.1 %copy-start.10 = (f32[8,128]{1,0:T(8,128)S(1)}, f32[8,128]{1,0:T(8,128)}, u32[]{:S(2)}) copy-start(f32[8,128]{1,0:T(8,128)} %param.9) | copy-start | bytes 12292
  47.8 16.0 %collective-permute-start.3 = (f32[32,16,512]{2,1,0:T(8,128)S(1)}, f32[32,16,512]{2,1,0:T(8,128)S(1)}, u32[]{:S(2)}, u32[]{:S(2)}) collective-permute-start(f32[32,16,512]{2,1,0:T(8,128)S(1)} %pad_maximum_fusion), channel_id=1, source_target_pairs={{0,112},{1,17},{2,114},{3,19},{4,116},{5,21},{6,118},{7,23},{8,120... | collective-permute-start | bytes 3145736 | tf_op jit(solution)/shard_map/ppermute | solution.py:24
  63.8 1.0 copy-start.3
  64.7 1.3 copy-start
  70.5 17.2 %collective-permute-start.4 = (f32[4,8,16,128]{3,2,1,0:T(8,128)}, f32[4,8,16,128]{3,2,1,0:T(8,128)S(1)}, u32[]{:S(2)}, u32[]{:S(2)}) collective-permute-start(f32[4,8,16,128]{3,2,1,0:T(8,128)} %get-tuple-element.12), channel_id=1, source_target_pairs={{0,2},{1,15},{2,4},{3,1},{4,6},{5,3},{6,8},{7,5},{8,10},{9,7},{10,... | collective-permute-start | bytes 786440 | tf_op jit(solution)/shard_map/ppermute | solution.py:24
  89.4 21.6 %all-to-all-start.3 = ((f32[32,16,128]{2,1,0:T(8,128)}), f32[32,16,128]{2,1,0:T(8,128)S(1)}, u32[]{:S(2)}, u32[]{:S(2)}) async-start(f32[32,16,128]{2,1,0:T(8,128)} %bitcast.2), calls=%async_computation.3 | async-start | bytes 524288 | tf_op jit(solution)/shard_map/all_to_all | solution.py:162
  111.1 24.0 %copy-start.4 = (f32[32,16,128]{2,1,0:T(8,128)}, f32[32,16,128]{2,1,0:T(8,128)S(1)}, u32[]{:S(2)}) copy-start(f32[32,16,128]{2,1,0:T(8,128)S(1)} %all-to-all-done.3) | copy-start | bytes 786436
  111.1 24.0 %all-to-all-start.2 = ((f32[64,16,128]{2,1,0:T(8,128)}), f32[64,16,128]{2,1,0:T(8,128)S(1)}, u32[]{:S(2)}, u32[]{:S(2)}) async-start(f32[64,16,128]{2,1,0:T(8,128)} %bitcast.9), calls=%async_computation.2 | async-start | bytes 1048576 | tf_op jit(solution)/shard_map/all_to_all | solution.py:157
  135.1 0.8 copy-start.2

commit v3 on v1

v3 whole, which is shorter than its diff:
```python
import jax
import jax.numpy as jnp
import numpy as np
from jax import lax
from jax.experimental import pallas as pl
from jax.experimental.pallas import tpu as pltpu
from jax.sharding import Mesh, PartitionSpec as P

IRREPS = 8
SLOTS = 128
NX, NY, NZ, NC = 4, 8, 8, 2
AXES = ("x", "y", "z", "c")
K_LOCAL = 512
OFFSETS = (0, 1, 7, 2, 6, 3, 5, 4)


IDS = np.arange(NX * NY * NZ * NC).reshape(NX, NY, NZ, NC)


def send(value, axis, first, second):
    targets = np.stack([np.roll(IDS[..., 0], -first, axis=axis), np.roll(IDS[..., 1], -second, axis=axis)], axis=-1)
    return lax.ppermute(value, AXES, list(zip(IDS.ravel().tolist(), targets.ravel().tolist())))


def split(value):
    high = value.astype(jnp.bfloat16)
    low = (value - high.astype(jnp.float32)).astype(jnp.bfloat16)
    return high, low


def product_body(occ_ref, count_ref, *refs):
    *t_refs, w_ref, out_ref, t_high, t_low, w_high, w_low = refs
    y = lax.axis_index("y")
    z = lax.axis_index("z")
    g = lax.axis_index("x") * NC + lax.axis_index("c")
    for slot, ref in enumerate(t_refs):
        for i in range(NX):
            for c in range(NC):
                high, low = split(ref[i * NC + c])
                rows = pl.ds((slot * NX + i) * 16, 16)
                cols = pl.ds(c * K_LOCAL, K_LOCAL)
                t_high[rows, cols] = high
                t_low[rows, cols] = low

    slots = lax.broadcasted_iota(jnp.int32, (SLOTS, SLOTS), 0)
    for c in range(NC):
        for k in range(4):
            live = slots < count_ref[jnp.bitwise_xor(occ_ref[z * 8 + c * 4 + k], g)]
            for col in range(NX):
                part = jnp.where(live, w_ref[col * NC + c, pl.ds(k * SLOTS, SLOTS), :], 0.0)
                high, low = split(part)
                rows = pl.ds(c * K_LOCAL + k * SLOTS, SLOTS)
                cols = pl.ds(col * SLOTS, SLOTS)
                w_high[rows, cols] = high
                w_low[rows, cols] = low

    def dot(a, b):
        return jnp.dot(a[...], b[...], preferred_element_type=jnp.float32)

    total = dot(t_high, w_low) + dot(t_low, w_high) + dot(t_high, w_high)
    for slot, offset in enumerate(OFFSETS):
        first = pl.multiple_of(lax.rem(y + offset, NY) * 16, 16)
        for i in range(NX):
            rows = slice((slot * NX + i) * 16, (slot * NX + i + 1) * 16)
            for col in range(NX):
                out_ref[col, i, pl.ds(first, 16), :] = total[rows, col * SLOTS : (col + 1) * SLOTS]


def product(occ_irrep, vir_count, blocks, w):
    return pl.pallas_call(
        product_body,
        in_specs=[pl.BlockSpec(memory_space=pltpu.SMEM)] * 2
        + [pl.BlockSpec(memory_space=pltpu.VMEM)] * (len(blocks) + 1),
        out_shape=jax.ShapeDtypeStruct((NX, NX, SLOTS, SLOTS), jnp.float32),
        scratch_shapes=[
            pltpu.VMEM((512, 2 * K_LOCAL), jnp.bfloat16),
            pltpu.VMEM((512, 2 * K_LOCAL), jnp.bfloat16),
            pltpu.VMEM((2 * K_LOCAL, NX * SLOTS), jnp.bfloat16),
            pltpu.VMEM((2 * K_LOCAL, NX * SLOTS), jnp.bfloat16),
        ],
        name="product",
    )(occ_irrep, vir_count, *blocks, pltpu.with_memory_space_constraint(w, pltpu.VMEM))


def finish_body(parts_ref, factor_ref, out_ref):
    for x in range(NX):
        for c in range(NC):
            total = parts_ref[x, 0, c]
            for z in range(1, NZ):
                total = total + parts_ref[x, z, c]
            out_ref[x * NC + c] = total * factor_ref[x * NC + c]


def finish(parts, factor):
    return pl.pallas_call(
        finish_body,
        in_specs=[pl.BlockSpec(memory_space=pltpu.VMEM)] * 2,
        out_shape=jax.ShapeDtypeStruct((IRREPS, 32, SLOTS), jnp.float32),
        name="finish",
    )(pltpu.with_memory_space_constraint(parts, pltpu.VMEM), factor)


def factors(occ_energy, vir_energy, occ_irrep, vir_count):
    row_i = lax.axis_index("z") // 2
    row_a = (lax.axis_index("z") % 2 * NC + lax.axis_index("c")) * 32
    col_j = lax.axis_index("x") * NY + lax.axis_index("y")
    irreps = jnp.arange(IRREPS, dtype=jnp.int32)
    slots = jnp.arange(SLOTS, dtype=jnp.int32)

    def side(occupied):
        label = jnp.bitwise_xor(lax.dynamic_index_in_dim(occ_irrep, occupied, 0, False), irreps)
        onehot = label[:, None] == irreps[None, :]
        count = jnp.sum(jnp.where(onehot, vir_count[None, :], 0), axis=1)
        energy = jnp.sum(jnp.where(onehot[:, :, None], vir_energy[None], 0.0), axis=1)
        energy = lax.dynamic_index_in_dim(occ_energy, occupied, 0, False) - energy
        return energy, (slots[None, :] < count[:, None]).astype(jnp.float32)

    e_row, m_row = side(row_i)
    e_col, m_col = side(col_j)
    e_row = lax.dynamic_slice_in_dim(e_row, row_a, 32, 1)
    m_row = lax.dynamic_slice_in_dim(m_row, row_a, 32, 1)
    return m_row[:, :, None] * m_col[:, None, :] / (e_row[:, :, None] + e_col[:, None, :])


def on_device(t_cycle, w_cycle, occ_energy, vir_energy, occ_irrep, vir_count):
    own = lax.all_to_all(t_cycle, ("x", "c"), 0, 0, tiled=True)
    w_cycle, own = lax.optimization_barrier((w_cycle, own))
    w = lax.all_to_all(w_cycle, ("x", "c"), 0, 0, tiled=True)
    across = send(own, 1, 4, 4)
    blocks, up, down = [own], own, own
    for _ in range(3):
        up = send(up, 1, -1, -1)
        down = send(down, 1, 1, 1)
        blocks += [up, down]
    blocks.append(across)
    partial = product(occ_irrep, vir_count, blocks, w)
    parts = lax.all_to_all(partial.reshape(NX * NZ * NC, 32, SLOTS), ("x", "z", "c"), 0, 0, tiled=True)
    factor = factors(occ_energy, vir_energy, occ_irrep, vir_count)
    return finish(parts.reshape(NX, NZ, NC, 32, SLOTS), factor)


def solution(mesh):
    grid = Mesh(mesh.devices.reshape(NX, NY, NZ, NC), AXES)
    return jax.shard_map(
        on_device,
        mesh=grid,
        in_specs=(P(None, ("x", "y"), ("z", "c")), P(None, ("z", "c"), ("x", "y")), P(), P(), P(), P()),
        out_specs=P(None, ("z", "c"), ("x", "y")),
        check_vma=False,
    )
```

time: 117 us -> 116 us (level)
  starting transfers between devices: 33.2 us -> 44.7 us
  waiting for transfers between devices: 51 us -> 40.4 us
  local copies, waits for them, and re-layouts: 4.58 us -> 2.88 us
    ppermute x5 -> x7, waiting for transfers between devices: 27.8 us -> 17.3 us  [send(): lax.ppermute(value, AXES, list(zip(IDS.ravel().tolist(), targets.ravel()....]
    ppermute x5 -> x7, starting transfers between devices: 13.6 us -> 20.4 us  [send(): lax.ppermute(value, AXES, list(zip(IDS.ravel().tolist(), targets.ravel()....]
    all_to_all x1, starting transfers between devices: 15.1 us -> 19.8 us  [on_device(): lax.all_to_all(partial.reshape(NX * NZ * NC, 32, SLOTS), ('x', 'z', 'c'),...]
    unnamed x22, local copies, waits for them, and re-layouts: 3.15 us -> 1.45 us
  transfers between devices with their start and end apart: 7 -> 9, of which waited for: 6 -> 6; matrix products, arithmetic and copies ran while one was open for 5% -> 5% of each run, Pallas kernels for 0% -> 0%
where the time goes in v3:
time: 116 us; the launch traced here: 115 us
  starting transfers between devices  44.7 us (39%)
  waiting for transfers between devices  40.4 us (35%)
  blocking collectives  16.6 us (14%)
  Pallas kernels  6.09 us (5%)
  other arithmetic  3.89 us (3%)
  local copies, waits for them, and re-layouts  2.88 us (2%)
    all_to_all x1, waiting for transfers between devices, on_device(): lax.all_to_all(partial.reshape(NX * NZ * NC, 32, SLOTS), ('x', 'z', 'c'),...  23.1 us
    ppermute x7, starting transfers between devices, send(): lax.ppermute(value, AXES, list(zip(IDS.ravel().tolist(), targets.ravel()....  20.4 us
    all_to_all x1, starting transfers between devices, on_device(): lax.all_to_all(partial.reshape(NX * NZ * NC, 32, SLOTS), ('x', 'z', 'c'),...  19.8 us
    ppermute x7, waiting for transfers between devices, send(): lax.ppermute(value, AXES, list(zip(IDS.ravel().tolist(), targets.ravel()....  17.3 us
    all_to_all x1, blocking collectives, on_device(): own = lax.all_to_all(t_cycle, ('x', 'c'), 0, 0, tiled=True)  16.6 us
    all_to_all x1, starting transfers between devices, on_device(): w = lax.all_to_all(w_cycle, ('x', 'c'), 0, 0, tiled=True)  4.55 us
    pallas_call x1, Pallas kernels, product(): pl.pallas_call(product_body, in_specs=[pl.BlockSpec(memory_space=pltpu.SM...  4.48 us
  transfers between devices with their start and end apart: 9, of which 6 were waited for; matrix products, arithmetic and copies ran while one was open for 5% of the time, Pallas kernels for 0%

profile of v3, /device:TPU:1, one launch (start us, length us, event | category | flops | bytes accessed | tf_op | source)
XLA Modules:
  0.0 114.9 jit_solution(13823216481992085463)
XLA Ops:
  0.0 16.6 %all_to_all.15.refs_0_ = f32[8,16,512]{2,1,0:T(8,128)S(1)} all-to-all(f32[8,16,512]{2,1,0:T(8,128)} %param.6), channel_id=1, replica_groups=mesh['x'=4,'y'=8,'z'=8,'c'=2] {'x','c'}, dimensions={0} | all-to-all | bytes 524288 | tf_op jit(solution)/shard_map/all_to_all | solution.py:126
  16.6 0.0 copy-start
  16.6 4.5 %all-to-all-start.1 = ((f32[8,512,128]{2,1,0:T(8,128)}), f32[8,512,128]{2,1,0:T(8,128)S(1)}, u32[]{:S(2)}, u32[]{:S(2)}) async-start(f32[8,512,128]{2,1,0:T(8,128)} %param.7), calls=%async_computation.1 | async-start | bytes 4194304 | tf_op jit(solution)/shard_map/all_to_all | solution.py:128
  21.2 1.9 %collective-permute-start = (f32[8,16,512]{2,1,0:T(8,128)S(1)}, f32[8,16,512]{2,1,0:T(8,128)S(1)}, u32[]{:S(2)}, u32[]{:S(2)}) collective-permute-start(f32[8,16,512]{2,1,0:T(8,128)S(1)} %all_to_all.15.refs_0_), channel_id=1, source_target_pairs={{0,112},{1,113},{2,114},{3,115},{4,116},{5,117},{6,118},{7,119},{8... | collective-permute-start | bytes 786440 | tf_op jit(solution)/shard_map/ppermute | solution.py:22
  23.1 3.4 %collective-permute-start.1 = (f32[8,16,512]{2,1,0:T(8,128)S(1)}, f32[8,16,512]{2,1,0:T(8,128)S(1)}, u32[]{:S(2)}, u32[]{:S(2)}) collective-permute-start(f32[8,16,512]{2,1,0:T(8,128)S(1)} %all_to_all.15.refs_0_), channel_id=1, source_target_pairs={{0,16},{1,17},{2,18},{3,19},{4,20},{5,21},{6,22},{7,23},{8,24},{9,... | collective-permute-start | bytes 786440 | tf_op jit(solution)/shard_map/ppermute | solution.py:22
  26.5 4.3 %collective-permute-done.refs_1_ = f32[8,16,512]{2,1,0:T(8,128)S(1)} collective-permute-done((f32[8,16,512]{2,1,0:T(8,128)S(1)}, f32[8,16,512]{2,1,0:T(8,128)S(1)}, u32[]{:S(2)}, u32[]{:S(2)}) %collective-permute-start) | collective-permute-done | bytes 262176 | tf_op jit(solution)/shard_map/ppermute | solution.py:22
  30.8 0.0 copy-start.1
  30.8 3.4 %collective-permute-start.2 = (f32[8,16,512]{2,1,0:T(8,128)S(1)}, f32[8,16,512]{2,1,0:T(8,128)S(1)}, u32[]{:S(2)}, u32[]{:S(2)}) collective-permute-start(f32[8,16,512]{2,1,0:T(8,128)S(1)} %collective-permute-done.refs_1_), channel_id=1, source_target_pairs={{0,112},{1,113},{2,114},{3,115},{4,116},{5,117},{6,118},{7,119},{8... | collective-permute-start | bytes 786440 | tf_op jit(solution)/shard_map/ppermute | solution.py:22
  34.2 0.0 collective-permute-done.1.refs_2_
  34.2 0.0 copy-start.2
  34.2 1.9 %collective-permute-start.3 = (f32[8,16,512]{2,1,0:T(8,128)S(1)}, f32[8,16,512]{2,1,0:T(8,128)S(1)}, u32[]{:S(2)}, u32[]{:S(2)}) collective-permute-start(f32[8,16,512]{2,1,0:T(8,128)S(1)} %collective-permute-done.1.refs_2_), channel_id=1, source_target_pairs={{0,16},{1,17},{2,18},{3,19},{4,20},{5,21},{6,22},{7,23},{8,24},{9,... | collective-permute-start | bytes 786440 | tf_op jit(solution)/shard_map/ppermute | solution.py:22
  36.2 0.0 copy-done
  36.2 3.0 %collective-permute-start.6 = (f32[8,16,512]{2,1,0:T(8,128)S(1)}, f32[8,16,512]{2,1,0:T(8,128)S(1)}, u32[]{:S(2)}, u32[]{:S(2)}) collective-permute-start(f32[8,16,512]{2,1,0:T(8,128)S(1)} %all_to_all.15.refs_0_), channel_id=1, source_target_pairs={{0,64},{1,65},{2,66},{3,67},{4,68},{5,69},{6,70},{7,71},{8,72},{9,... | collective-permute-start | bytes 786440 | tf_op jit(solution)/shard_map/ppermute | solution.py:22
  39.2 0.4 collective-permute-done.2.refs_3_
  39.6 0.0 copy-start.3
  39.6 4.9 %collective-permute-start.4 = (f32[8,16,512]{2,1,0:T(8,128)S(1)}, f32[8,16,512]{2,1,0:T(8,128)S(1)}, u32[]{:S(2)}, u32[]{:S(2)}) collective-permute-start(f32[8,16,512]{2,1,0:T(8,128)S(1)} %collective-permute-done.2.refs_3_), channel_id=1, source_target_pairs={{0,112},{1,113},{2,114},{3,115},{4,116},{5,117},{6,118},{7,119},{8... | collective-permute-start | bytes 786440 | tf_op jit(solution)/shard_map/ppermute | solution.py:22
  44.5 7.5 %collective-permute-done.3.refs_4_ = f32[8,16,512]{2,1,0:T(8,128)S(1)} collective-permute-done((f32[8,16,512]{2,1,0:T(8,128)S(1)}, f32[8,16,512]{2,1,0:T(8,128)S(1)}, u32[]{:S(2)}, u32[]{:S(2)}) %collective-permute-start.3) | collective-permute-done | bytes 262176 | tf_op jit(solution)/shard_map/ppermute | solution.py:22
  52.0 0.0 copy-start.4
  52.0 1.9 %collective-permute-start.5 = (f32[8,16,512]{2,1,0:T(8,128)S(1)}, f32[8,16,512]{2,1,0:T(8,128)}, u32[]{:S(2)}, u32[]{:S(2)}) collective-permute-start(f32[8,16,512]{2,1,0:T(8,128)S(1)} %collective-permute-done.3.refs_4_), channel_id=1, source_target_pairs={{0,16},{1,17},{2,18},{3,19},{4,20},{5,21},{6,22},{7,23},{8,24},{9,... | collective-permute-start | bytes 786440 | tf_op jit(solution)/shard_map/ppermute | solution.py:22
  53.9 0.3 collective-permute-done.6.refs_7_
  54.2 0.0 copy-start.5
  54.2 0.0 collective-permute-done.4.refs_5_
  54.2 0.7 copy-done.5
  54.9 0.0 copy-start.6
  54.9 0.7 copy-done.6
  55.6 4.8 %collective-permute-done.5.refs_6_ = f32[8,16,512]{2,1,0:T(8,128)} collective-permute-done((f32[8,16,512]{2,1,0:T(8,128)S(1)}, f32[8,16,512]{2,1,0:T(8,128)}, u32[]{:S(2)}, u32[]{:S(2)}) %collective-permute-start.5) | collective-permute-done | bytes 262176 | tf_op jit(solution)/shard_map/ppermute | solution.py:22
  60.4 0.0 all-to-all-done.1.refs_8_
  60.4 0.0 copy-done.1
  60.4 0.0 copy-done.2
  60.4 0.0 copy-done.3
  60.4 0.0 copy-done.4
  60.4 4.5 %product.1 = f32[4,4,128,128]{3,2,1,0:T(8,128)} custom-call(s32[64]{0:T(128)} %occ_ref.1, s32[8]{0:T(128)} %count_ref.1, f32[8,16,512]{2,1,0:T(8,128)} %copy-done, f32[8,16,512]{2,1,0:T(8,128)} %copy-done.1, f32[8,16,512]{2,1,0:T(8,128)} %copy-done.2, f32[8,16,512]{2,1,0:T(8,128)} %copy-done.3, f32[8,16,512]{2,1,0:T(8,128)} %copy-done.4, ...), custom_call_target="tpu_custom_call" | custom-call | tf_op jit(solution)/shard_map/product/pallas_call | solution.py:70
  64.9 0.0 copy-start.7
  64.9 0.0 copy-start.10
  64.9 0.0 copy-start.8
  64.9 0.0 copy-start.9
  64.9 19.8 %all-to-all-start.2 = ((f32[64,32,128]{2,1,0:T(8,128)}), f32[64,32,128]{2,1,0:T(8,128)S(1)}, u32[]{:S(2)}, u32[]{:S(2)}) async-start(f32[64,32,128]{2,1,0:T(8,128)} %bitcast.7), calls=%async_computation.2 | async-start | bytes 2097152 | tf_op jit(solution)/shard_map/all_to_all | solution.py:137
  84.7 0.0 copy-done.7
  84.8 0.6 fusion.3
  85.4 0.0 copy-done.10
  85.4 0.7 fusion.2
  86.0 0.6 iota_xor_fusion
  86.7 0.6 iota_xor_fusion.1
  87.3 0.1 iota_compare_fusion
  87.4 0.0 copy-done.8
  87.4 0.1 select_reduce_fusion.1
  87.5 0.6 broadcast_subtract_fusion.1
  88.1 0.1 constant_dynamic-slice_fusion.1
  88.2 0.0 copy-done.9
  88.2 0.2 select_reduce_fusion.3
  88.4 0.1 fusion
  88.5 0.1 constant_dynamic-slice_fusion
  88.6 0.1 fusion.1
  88.7 0.7 broadcast_subtract_fusion
  89.3 0.8 add_divide_fusion.factor_ref
  90.1 23.1 %all-to-all-done.2 = f32[64,32,128]{2,1,0:T(8,128)S(1)} async-done(((f32[64,32,128]{2,1,0:T(8,128)}), f32[64,32,128]{2,1,0:T(8,128)S(1)}, u32[]{:S(2)}, u32[]{:S(2)}) %all-to-all-start.2) | async-done | bytes 1048608 | tf_op jit(solution)/shard_map/all_to_all | solution.py:137
  113.2 1.6 %finish.1 = f32[8,32,128]{2,1,0:T(8,128)} custom-call(f32[4,8,2,32,128]{4,3,2,1,0:T(8,128)S(1)} %bitcast.6, f32[8,32,128]{2,1,0:T(8,128)} %add_divide_fusion.factor_ref), custom_call_target="tpu_custom_call" | custom-call | tf_op jit(solution)/shard_map/finish/pallas_call | solution.py:95
Async XLA Ops:
  16.6 19.5 %copy-start = (f32[8,16,512]{2,1,0:T(8,128)}, f32[8,16,512]{2,1,0:T(8,128)S(1)}, u32[]{:S(2)}) copy-start(f32[8,16,512]{2,1,0:T(8,128)S(1)} %all_to_all.15.refs_0_) | copy-start | bytes 786436
  16.6 43.8 %all-to-all-start.1 = ((f32[8,512,128]{2,1,0:T(8,128)}), f32[8,512,128]{2,1,0:T(8,128)S(1)}, u32[]{:S(2)}, u32[]{:S(2)}) async-start(f32[8,512,128]{2,1,0:T(8,128)} %param.7), calls=%async_computation.1 | async-start | bytes 4194304 | tf_op jit(solution)/shard_map/all_to_all | solution.py:128
  21.2 9.6 %collective-permute-start = (f32[8,16,512]{2,1,0:T(8,128)S(1)}, f32[8,16,512]{2,1,0:T(8,128)S(1)}, u32[]{:S(2)}, u32[]{:S(2)}) collective-permute-start(f32[8,16,512]{2,1,0:T(8,128)S(1)} %all_to_all.15.refs_0_), channel_id=1, source_target_pairs={{0,112},{1,113},{2,114},{3,115},{4,116},{5,117},{6,118},{7,119},{8... | collective-permute-start | bytes 786440 | tf_op jit(solution)/shard_map/ppermute | solution.py:22
  23.1 11.1 %collective-permute-start.1 = (f32[8,16,512]{2,1,0:T(8,128)S(1)}, f32[8,16,512]{2,1,0:T(8,128)S(1)}, u32[]{:S(2)}, u32[]{:S(2)}) collective-permute-start(f32[8,16,512]{2,1,0:T(8,128)S(1)} %all_to_all.15.refs_0_), channel_id=1, source_target_pairs={{0,16},{1,17},{2,18},{3,19},{4,20},{5,21},{6,22},{7,23},{8,24},{9,... | collective-permute-start | bytes 786440 | tf_op jit(solution)/shard_map/ppermute | solution.py:22
  30.8 29.6 %copy-start.1 = (f32[8,16,512]{2,1,0:T(8,128)}, f32[8,16,512]{2,1,0:T(8,128)S(1)}, u32[]{:S(2)}) copy-start(f32[8,16,512]{2,1,0:T(8,128)S(1)} %collective-permute-done.refs_1_) | copy-start | bytes 786436
  30.8 8.8 %collective-permute-start.2 = (f32[8,16,512]{2,1,0:T(8,128)S(1)}, f32[8,16,512]{2,1,0:T(8,128)S(1)}, u32[]{:S(2)}, u32[]{:S(2)}) collective-permute-start(f32[8,16,512]{2,1,0:T(8,128)S(1)} %collective-permute-done.refs_1_), channel_id=1, source_target_pairs={{0,112},{1,113},{2,114},{3,115},{4,116},{5,117},{6,118},{7,119},{8... | collective-permute-start | bytes 786440 | tf_op jit(solution)/shard_map/ppermute | solution.py:22
  34.2 26.2 %copy-start.2 = (f32[8,16,512]{2,1,0:T(8,128)}, f32[8,16,512]{2,1,0:T(8,128)S(1)}, u32[]{:S(2)}) copy-start(f32[8,16,512]{2,1,0:T(8,128)S(1)} %collective-permute-done.1.refs_2_) | copy-start | bytes 786436
  34.2 17.8 %collective-permute-start.3 = (f32[8,16,512]{2,1,0:T(8,128)S(1)}, f32[8,16,512]{2,1,0:T(8,128)S(1)}, u32[]{:S(2)}, u32[]{:S(2)}) collective-permute-start(f32[8,16,512]{2,1,0:T(8,128)S(1)} %collective-permute-done.1.refs_2_), channel_id=1, source_target_pairs={{0,16},{1,17},{2,18},{3,19},{4,20},{5,21},{6,22},{7,23},{8,24},{9,... | collective-permute-start | bytes 786440 | tf_op jit(solution)/shard_map/ppermute | solution.py:22
  36.2 18.0 %collective-permute-start.6 = (f32[8,16,512]{2,1,0:T(8,128)S(1)}, f32[8,16,512]{2,1,0:T(8,128)S(1)}, u32[]{:S(2)}, u32[]{:S(2)}) collective-permute-start(f32[8,16,512]{2,1,0:T(8,128)S(1)} %all_to_all.15.refs_0_), channel_id=1, source_target_pairs={{0,64},{1,65},{2,66},{3,67},{4,68},{5,69},{6,70},{7,71},{8,72},{9,... | collective-permute-start | bytes 786440 | tf_op jit(solution)/shard_map/ppermute | solution.py:22
  39.6 20.9 %copy-start.3 = (f32[8,16,512]{2,1,0:T(8,128)}, f32[8,16,512]{2,1,0:T(8,128)S(1)}, u32[]{:S(2)}) copy-start(f32[8,16,512]{2,1,0:T(8,128)S(1)} %collective-permute-done.2.refs_3_) | copy-start | bytes 786436
  39.6 14.6 %collective-permute-start.4 = (f32[8,16,512]{2,1,0:T(8,128)S(1)}, f32[8,16,512]{2,1,0:T(8,128)S(1)}, u32[]{:S(2)}, u32[]{:S(2)}) collective-permute-start(f32[8,16,512]{2,1,0:T(8,128)S(1)} %collective-permute-done.2.refs_3_), channel_id=1, source_target_pairs={{0,112},{1,113},{2,114},{3,115},{4,116},{5,117},{6,118},{7,119},{8... | collective-permute-start | bytes 786440 | tf_op jit(solution)/shard_map/ppermute | solution.py:22
  52.0 8.4 %copy-start.4 = (f32[8,16,512]{2,1,0:T(8,128)}, f32[8,16,512]{2,1,0:T(8,128)S(1)}, u32[]{:S(2)}) copy-start(f32[8,16,512]{2,1,0:T(8,128)S(1)} %collective-permute-done.3.refs_4_) | copy-start | bytes 786436
  52.0 8.4 %collective-permute-start.5 = (f32[8,16,512]{2,1,0:T(8,128)S(1)}, f32[8,16,512]{2,1,0:T(8,128)}, u32[]{:S(2)}, u32[]{:S(2)}) collective-permute-start(f32[8,16,512]{2,1,0:T(8,128)S(1)} %collective-permute-done.3.refs_4_), channel_id=1, source_target_pairs={{0,16},{1,17},{2,18},{3,19},{4,20},{5,21},{6,22},{7,23},{8,24},{9,... | collective-permute-start | bytes 786440 | tf_op jit(solution)/shard_map/ppermute | solution.py:22
  54.2 0.7 copy-start.5
  54.9 0.7 copy-start.6
  64.9 19.8 %copy-start.7 = (s32[64]{0:T(128)S(1)}, s32[64]{0:T(128)}, u32[]{:S(2)}) copy-start(s32[64]{0:T(128)} %occ_ref.1) | copy-start | bytes 772
  64.9 20.5 %copy-start.10 = (f32[64]{0:T(128)S(1)}, f32[64]{0:T(128)}, u32[]{:S(2)}) copy-start(f32[64]{0:T(128)} %param.8) | copy-start | bytes 772
  64.9 22.5 %copy-start.8 = (f32[8,128]{1,0:T(8,128)S(1)}, f32[8,128]{1,0:T(8,128)}, u32[]{:S(2)}) copy-start(f32[8,128]{1,0:T(8,128)} %param.9) | copy-start | bytes 12292
  64.9 23.3 %copy-start.9 = (s32[8]{0:T(128)S(1)}, s32[8]{0:T(128)}, u32[]{:S(2)}) copy-start(s32[8]{0:T(128)} %count_ref.1) | copy-start | bytes 100
  64.9 48.3 %all-to-all-start.2 = ((f32[64,32,128]{2,1,0:T(8,128)}), f32[64,32,128]{2,1,0:T(8,128)S(1)}, u32[]{:S(2)}, u32[]{:S(2)}) async-start(f32[64,32,128]{2,1,0:T(8,128)} %bitcast.7), calls=%async_computation.2 | async-start | bytes 2097152 | tf_op jit(solution)/shard_map/all_to_all | solution.py:137

commit v4 on v3

--- a/solution.py
+++ b/solution.py
@@ -11,7 +11,7 @@
 NX, NY, NZ, NC = 4, 8, 8, 2
 AXES = ("x", "y", "z", "c")
 K_LOCAL = 512
-OFFSETS = (0, 1, 7, 2, 6, 3, 5, 4)
+OFFSETS = (0, 1, 7, 4, 2, 5, 6, 3)
 
 
 IDS = np.arange(NX * NY * NZ * NC).reshape(NX, NY, NZ, NC)
@@ -28,20 +28,32 @@
     return high, low
 
 
-def product_body(occ_ref, count_ref, *refs):
-    *t_refs, w_ref, out_ref, t_high, t_low, w_high, w_low = refs
+def split_rows(t_in, t_high, t_low):
+    for n in range(4):
+        for i in range(NX):
+            for c in range(NC):
+                high, low = split(t_in[n * 8 + i * NC + c])
+                rows = pl.ds((n * NX + i) * 16, 16)
+                cols = pl.ds(c * K_LOCAL, K_LOCAL)
+                t_high[rows, cols] = high
+                t_low[rows, cols] = low
+
+
+def multiply(t_high, t_low, w_high, w_low):
+    def dot(a, b):
+        return jnp.dot(a[...], b[...], preferred_element_type=jnp.float32)
+
+    return dot(t_high, w_low) + dot(t_low, w_high) + dot(t_high, w_high)
+
+
+def first_body(occ_ref, count_ref, *refs):
+    *t_refs, w_ref, out_ref, w_high, w_low, t_in, t_high, t_low, sems = refs
     y = lax.axis_index("y")
     z = lax.axis_index("z")
     g = lax.axis_index("x") * NC + lax.axis_index("c")
-    for slot, ref in enumerate(t_refs):
-        for i in range(NX):
-            for c in range(NC):
-                high, low = split(ref[i * NC + c])
-                rows = pl.ds((slot * NX + i) * 16, 16)
-                cols = pl.ds(c * K_LOCAL, K_LOCAL)
-                t_high[rows, cols] = high
-                t_low[rows, cols] = low
-
+    copies = [pltpu.make_async_copy(ref, t_in.at[pl.ds(n * 8, 8)], sems.at[n]) for n, ref in enumerate(t_refs)]
+    for copy in copies:
+        copy.start()
     slots = lax.broadcasted_iota(jnp.int32, (SLOTS, SLOTS), 0)
     for c in range(NC):
         for k in range(4):
@@ -53,33 +65,73 @@
                 cols = pl.ds(col * SLOTS, SLOTS)
                 w_high[rows, cols] = high
                 w_low[rows, cols] = low
-
-    def dot(a, b):
-        return jnp.dot(a[...], b[...], preferred_element_type=jnp.float32)
-
-    total = dot(t_high, w_low) + dot(t_low, w_high) + dot(t_high, w_high)
-    for slot, offset in enumerate(OFFSETS):
-        first = pl.multiple_of(lax.rem(y + offset, NY) * 16, 16)
+    for copy in copies:
+        copy.wait()
+    split_rows(t_in, t_high, t_low)
+    total = multiply(t_high, t_low, w_high, w_low)
+    for n in range(4):
+        first = pl.multiple_of(lax.rem(y + OFFSETS[n], NY) * 16, 16)
         for i in range(NX):
-            rows = slice((slot * NX + i) * 16, (slot * NX + i + 1) * 16)
             for col in range(NX):
+                rows = slice((n * NX + i) * 16, (n * NX + i + 1) * 16)
                 out_ref[col, i, pl.ds(first, 16), :] = total[rows, col * SLOTS : (col + 1) * SLOTS]
 
 
+def second_body(partial_ref, t0, t1, w_high, w_low, out_ref, t_in, t_high, t_low, rows_out, sems):
+    del partial_ref
+    y = lax.axis_index("y")
+    t_copies = [pltpu.make_async_copy(ref, t_in.at[pl.ds(n * 16, 16)], sems.at[n]) for n, ref in enumerate((t0, t1))]
+    for copy in t_copies:
+        copy.start()
+    for copy in t_copies:
+        copy.wait()
+    split_rows(t_in, t_high, t_low)
+    total = multiply(t_high, t_low, w_high, w_low)
+    out_copies = []
+    for n in range(4):
+        first = pl.multiple_of(lax.rem(y + OFFSETS[4 + n], NY) * 16, 16)
+        for i in range(NX):
+            for col in range(NX):
+                rows = slice((n * NX + i) * 16, (n * NX + i + 1) * 16)
+                rows_out[n, col, i] = total[rows, col * SLOTS : (col + 1) * SLOTS]
+        out_copies.append(pltpu.make_async_copy(rows_out.at[n], out_ref.at[:, :, pl.ds(first, 16), :], sems.at[2 + n]))
+        out_copies[-1].start()
+    for copy in out_copies:
+        copy.wait()
+
+
 def product(occ_irrep, vir_count, blocks, w):
+    anywhere = pl.BlockSpec(memory_space=pl.ANY)
+    shape = jax.ShapeDtypeStruct((NX, NX, SLOTS, SLOTS), jnp.float32)
+    w_part = jax.ShapeDtypeStruct((2 * K_LOCAL, NX * SLOTS), jnp.bfloat16)
+    t_in = pltpu.VMEM((32, 16, K_LOCAL), jnp.float32)
+    t_part = pltpu.VMEM((256, 2 * K_LOCAL), jnp.bfloat16)
+    partial, w_high, w_low = pl.pallas_call(
+        first_body,
+        in_specs=[pl.BlockSpec(memory_space=pltpu.SMEM)] * 2
+        + [anywhere] * 4
+        + [pl.BlockSpec(memory_space=pltpu.VMEM)],
+        out_shape=(shape, w_part, w_part),
+        scratch_shapes=[t_in, t_part, t_part, pltpu.SemaphoreType.DMA((4,))],
+        name="first_product",
+    compiler_params=pltpu.CompilerParams(vmem_limit_bytes=20 * 2**20),
+    )(occ_irrep, vir_count, *blocks[:4], pltpu.with_memory_space_constraint(w, pltpu.VMEM))
     return pl.pallas_call(
-        product_body,
-        in_specs=[pl.BlockSpec(memory_space=pltpu.SMEM)] * 2
-        + [pl.BlockSpec(memory_space=pltpu.VMEM)] * (len(blocks) + 1),
-        out_shape=jax.ShapeDtypeStruct((NX, NX, SLOTS, SLOTS), jnp.float32),
+        second_body,
+        in_specs=[anywhere] * 3 + [pl.BlockSpec(memory_space=pltpu.VMEM)] * 2,
+        out_specs=anywhere,
+        out_shape=shape,
         scratch_shapes=[
-            pltpu.VMEM((512, 2 * K_LOCAL), jnp.bfloat16),
-            pltpu.VMEM((512, 2 * K_LOCAL), jnp.bfloat16),
-            pltpu.VMEM((2 * K_LOCAL, NX * SLOTS), jnp.bfloat16),
-            pltpu.VMEM((2 * K_LOCAL, NX * SLOTS), jnp.bfloat16),
+            t_in,
+            t_part,
+            t_part,
+            pltpu.VMEM((4, NX, NX, 16, SLOTS), jnp.float32),
+            pltpu.SemaphoreType.DMA((6,)),
         ],
-        name="product",
-    )(occ_irrep, vir_count, *blocks, pltpu.with_memory_space_constraint(w, pltpu.VMEM))
+        input_output_aliases={0: 0},
+        name="second_product",
+    compiler_params=pltpu.CompilerParams(vmem_limit_bytes=20 * 2**20),
+    )(partial, *blocks[4:], *[pltpu.with_memory_space_constraint(v, pltpu.VMEM) for v in (w_high, w_low)])
 
 
 def finish_body(parts_ref, factor_ref, out_ref):
@@ -97,6 +149,7 @@
         in_specs=[pl.BlockSpec(memory_space=pltpu.VMEM)] * 2,
         out_shape=jax.ShapeDtypeStruct((IRREPS, 32, SLOTS), jnp.float32),
         name="finish",
+        compiler_params=pltpu.CompilerParams(vmem_limit_bytes=16 * 2**20),
     )(pltpu.with_memory_space_constraint(parts, pltpu.VMEM), factor)
 
 
@@ -128,11 +181,11 @@
     w = lax.all_to_all(w_cycle, ("x", "c"), 0, 0, tiled=True)
     across = send(own, 1, 4, 4)
     blocks, up, down = [own], own, own
-    for _ in range(3):
-        up = send(up, 1, -1, -1)
-        down = send(down, 1, 1, 1)
-        blocks += [up, down]
-    blocks.append(across)
+    up = send(up, 1, -1, -1)
+    down = send(down, 1, 1, 1)
+    blocks += [up, down, across]
+    blocks.append(send(jnp.concatenate([up, across]), 1, -1, -1))
+    blocks.append(send(jnp.concatenate([down, across]), 1, 1, 1))
     partial = product(occ_irrep, vir_count, blocks, w)
     parts = lax.all_to_all(partial.reshape(NX * NZ * NC, 32, SLOTS), ("x", "z", "c"), 0, 0, tiled=True)
     factor = factors(occ_energy, vir_energy, occ_irrep, vir_count)

time: 116 us -> 113 us (0.974)
  starting transfers between devices: 44.7 us -> 33.2 us
  waiting for transfers between devices: 40.4 us -> 49.7 us
  local copies, waits for them, and re-layouts: 2.88 us -> 1.39 us
    ppermute x7 -> x5, waiting for transfers between devices: 17.3 us -> 25.8 us  [send(): lax.ppermute(value, AXES, list(zip(IDS.ravel().tolist(), targets.ravel()....]
    ppermute x7 -> x5, starting transfers between devices: 20.4 us -> 13.6 us  [send(): lax.ppermute(value, AXES, list(zip(IDS.ravel().tolist(), targets.ravel()....]
    all_to_all x1, starting transfers between devices: 19.8 us -> 14.9 us  [on_device(): lax.all_to_all(partial.reshape(NX * NZ * NC, 32, SLOTS), ('x', 'z', 'c'),...]
    pallas_call x1 -> x2, Pallas kernels: 4.48 us -> 6.04 us  [the longest x1 3.03 us: product(): pl.pallas_call(first_body, in_specs=[pl.BlockSpec(memory_space=pltpu.SMEM...]
    unnamed x22 -> x8, local copies, waits for them, and re-layouts: 1.45 us -> 0.02 us
  transfers between devices with their start and end apart: 9 -> 7, of which waited for: 6 -> 6; matrix products, arithmetic and copies ran while one was open for 5% -> 5% of each run, Pallas kernels for 0% -> 3%
where the time goes in v4:
time: 113 us; the launch traced here: 112 us
  waiting for transfers between devices  49.7 us (44%)
  starting transfers between devices  33.2 us (29%)
  blocking collectives  16.6 us (15%)
  Pallas kernels  6.76 us (6%)
  other arithmetic  4.3 us (4%)
  local copies, waits for them, and re-layouts  1.39 us (1%)
    ppermute x5, waiting for transfers between devices, send(): lax.ppermute(value, AXES, list(zip(IDS.ravel().tolist(), targets.ravel()....  25.8 us
    all_to_all x1, waiting for transfers between devices, on_device(): lax.all_to_all(partial.reshape(NX * NZ * NC, 32, SLOTS), ('x', 'z', 'c'),...  23.9 us
    all_to_all x1, blocking collectives, on_device(): own = lax.all_to_all(t_cycle, ('x', 'c'), 0, 0, tiled=True)  16.6 us
    all_to_all x1, starting transfers between devices, on_device(): lax.all_to_all(partial.reshape(NX * NZ * NC, 32, SLOTS), ('x', 'z', 'c'),...  14.9 us
    ppermute x5, starting transfers between devices, send(): lax.ppermute(value, AXES, list(zip(IDS.ravel().tolist(), targets.ravel()....  13.6 us
    all_to_all x1, starting transfers between devices, on_device(): w = lax.all_to_all(w_cycle, ('x', 'c'), 0, 0, tiled=True)  4.68 us
    pallas_call x1, Pallas kernels, product(): pl.pallas_call(first_body, in_specs=[pl.BlockSpec(memory_space=pltpu.SMEM...  3.03 us
    pallas_call x1, Pallas kernels, product(): pl.pallas_call(second_body, in_specs=[anywhere] * 3 + [pl.BlockSpec(memor...  3.01 us
  transfers between devices with their start and end apart: 7, of which 6 were waited for; matrix products, arithmetic and copies ran while one was open for 5% of the time, Pallas kernels for 3%

profile of v4, /device:TPU:1, one launch (start us, length us, event | category | flops | bytes accessed | tf_op | source)
XLA Modules:
  0.0 112.2 jit_solution(3237838550272080759)
XLA Ops:
  0.0 16.6 %all_to_all.15.refs_0_ = f32[8,16,512]{2,1,0:T(8,128)S(1)} all-to-all(f32[8,16,512]{2,1,0:T(8,128)} %param.6), channel_id=1, replica_groups=mesh['x'=4,'y'=8,'z'=8,'c'=2] {'x','c'}, dimensions={0} | all-to-all | bytes 524288 | tf_op jit(solution)/shard_map/all_to_all | solution.py:179
  16.6 0.0 copy-start
  16.6 0.0 copy-start.1
  16.6 4.7 %all-to-all-start.1 = ((f32[8,512,128]{2,1,0:T(8,128)}), f32[8,512,128]{2,1,0:T(8,128)S(1)}, u32[]{:S(2)}, u32[]{:S(2)}) async-start(f32[8,512,128]{2,1,0:T(8,128)} %param.7), calls=%async_computation.1 | async-start | bytes 4194304 | tf_op jit(solution)/shard_map/all_to_all | solution.py:181
  21.3 1.9 %collective-permute-start = (f32[8,16,512]{2,1,0:T(8,128)S(1)}, f32[8,16,512]{2,1,0:T(8,128)S(1)}, u32[]{:S(2)}, u32[]{:S(2)}) collective-permute-start(f32[8,16,512]{2,1,0:T(8,128)S(1)} %all_to_all.15.refs_0_), channel_id=1, source_target_pairs={{0,112},{1,113},{2,114},{3,115},{4,116},{5,117},{6,118},{7,119},{8... | collective-permute-start | bytes 786440 | tf_op jit(solution)/shard_map/ppermute | solution.py:22
  23.2 3.4 %collective-permute-start.1 = (f32[8,16,512]{2,1,0:T(8,128)S(1)}, f32[8,16,512]{2,1,0:T(8,128)S(1)}, u32[]{:S(2)}, u32[]{:S(2)}) collective-permute-start(f32[8,16,512]{2,1,0:T(8,128)S(1)} %all_to_all.15.refs_0_), channel_id=1, source_target_pairs={{0,16},{1,17},{2,18},{3,19},{4,20},{5,21},{6,22},{7,23},{8,24},{9,... | collective-permute-start | bytes 786440 | tf_op jit(solution)/shard_map/ppermute | solution.py:22
  26.6 3.1 %collective-permute-start.2 = (f32[8,16,512]{2,1,0:T(8,128)S(1)}, f32[8,16,512]{2,1,0:T(8,128)S(1)}, u32[]{:S(2)}, u32[]{:S(2)}) collective-permute-start(f32[8,16,512]{2,1,0:T(8,128)S(1)} %all_to_all.15.refs_0_), channel_id=1, source_target_pairs={{0,64},{1,65},{2,66},{3,67},{4,68},{5,69},{6,70},{7,71},{8,72},{9,... | collective-permute-start | bytes 786440 | tf_op jit(solution)/shard_map/ppermute | solution.py:22
  29.7 1.2 %collective-permute-done.refs_1_ = f32[8,16,512]{2,1,0:T(8,128)S(1)} collective-permute-done((f32[8,16,512]{2,1,0:T(8,128)S(1)}, f32[8,16,512]{2,1,0:T(8,128)S(1)}, u32[]{:S(2)}, u32[]{:S(2)}) %collective-permute-start) | collective-permute-done | bytes 262176 | tf_op jit(solution)/shard_map/ppermute | solution.py:22
  30.9 8.8 %collective-permute-done.1.refs_2_ = f32[8,16,512]{2,1,0:T(8,128)S(1)} collective-permute-done((f32[8,16,512]{2,1,0:T(8,128)S(1)}, f32[8,16,512]{2,1,0:T(8,128)S(1)}, u32[]{:S(2)}, u32[]{:S(2)}) %collective-permute-start.1) | collective-permute-done | bytes 262176 | tf_op jit(solution)/shard_map/ppermute | solution.py:22
  39.8 6.0 %collective-permute-done.2.refs_3_ = f32[8,16,512]{2,1,0:T(8,128)S(1)} collective-permute-done((f32[8,16,512]{2,1,0:T(8,128)S(1)}, f32[8,16,512]{2,1,0:T(8,128)S(1)}, u32[]{:S(2)}, u32[]{:S(2)}) %collective-permute-start.2) | collective-permute-done | bytes 262176 | tf_op jit(solution)/shard_map/ppermute | solution.py:22
  45.8 1.1 pad_maximum_fusion
  46.9 2.7 %collective-permute-start.3 = (f32[16,16,512]{2,1,0:T(8,128)}, f32[16,16,512]{2,1,0:T(8,128)}, u32[]{:S(2)}, u32[]{:S(2)}) collective-permute-start(f32[16,16,512]{2,1,0:T(8,128)} %get-tuple-element.20), channel_id=1, source_target_pairs={{0,112},{1,113},{2,114},{3,115},{4,116},{5,117},{6,118},{7,119},{8... | collective-permute-start | bytes 1572872 | tf_op jit(solution)/shard_map/ppermute | solution.py:22
  49.6 2.5 %collective-permute-start.4 = (f32[16,16,512]{2,1,0:T(8,128)}, f32[16,16,512]{2,1,0:T(8,128)}, u32[]{:S(2)}, u32[]{:S(2)}) collective-permute-start(f32[16,16,512]{2,1,0:T(8,128)} %get-tuple-element.19), channel_id=1, source_target_pairs={{0,16},{1,17},{2,18},{3,19},{4,20},{5,21},{6,22},{7,23},{8,24},{9,... | collective-permute-start | bytes 1572872 | tf_op jit(solution)/shard_map/ppermute | solution.py:22
  52.2 0.0 all-to-all-done.1.refs_4_
  52.2 0.0 copy-done
  52.2 0.0 copy-done.1
  52.2 3.0 %first_product.1 = (f32[4,4,128,128]{3,2,1,0:T(8,128)}, bf16[1024,512]{1,0:T(8,128)(2,1)S(1)}, bf16[1024,512]{1,0:T(8,128)(2,1)S(1)}) custom-call(s32[64]{0:T(128)S(1)} %copy-done, s32[8]{0:T(128)S(1)} %copy-done.1, f32[8,16,512]{2,1,0:T(8,128)S(1)} %all_to_all.15.refs_0_, f32[8,16,512]{2,1,0:T(8,128)S(1)} %collective-permute-done.refs_1_, ...), custom_call_target="tpu_custom_call" | custom-call | tf_op jit(solution)/shard_map/first_product/pallas_call | solution.py:109
  55.2 6.8 %collective-permute-done.3.t0 = f32[16,16,512]{2,1,0:T(8,128)} collective-permute-done((f32[16,16,512]{2,1,0:T(8,128)}, f32[16,16,512]{2,1,0:T(8,128)}, u32[]{:S(2)}, u32[]{:S(2)}) %collective-permute-start.3) | collective-permute-done | bytes 524320 | tf_op jit(solution)/shard_map/ppermute | solution.py:22
  62.0 2.9 %collective-permute-done.4.t1 = f32[16,16,512]{2,1,0:T(8,128)} collective-permute-done((f32[16,16,512]{2,1,0:T(8,128)}, f32[16,16,512]{2,1,0:T(8,128)}, u32[]{:S(2)}, u32[]{:S(2)}) %collective-permute-start.4) | collective-permute-done | bytes 524320 | tf_op jit(solution)/shard_map/ppermute | solution.py:22
  64.9 3.0 %second_product.1 = f32[4,4,128,128]{3,2,1,0:T(8,128)} custom-call(f32[4,4,128,128]{3,2,1,0:T(8,128)} %get-tuple-element.12.partial_ref, f32[16,16,512]{2,1,0:T(8,128)} %collective-permute-done.3.t0, f32[16,16,512]{2,1,0:T(8,128)} %collective-permute-done.4.t1, bf16[1024,512]{1,0:T(8,128)(2,1)S(1)} %get-tuple-element.13.w_high, ...), custom_call_target="tpu_custom_call", output_to_operand_aliasing={{}: (0, {})} | custom-call | tf_op jit(solution)/shard_map/second_product/pallas_call | solution.py:119
  68.0 0.0 copy-start.3
  68.0 0.0 copy-start.2
  68.0 14.9 %all-to-all-start.2 = ((f32[64,32,128]{2,1,0:T(8,128)}), f32[64,32,128]{2,1,0:T(8,128)S(1)}, u32[]{:S(2)}, u32[]{:S(2)}) async-start(f32[64,32,128]{2,1,0:T(8,128)} %bitcast), calls=%async_computation.2 | async-start | bytes 2097152 | tf_op jit(solution)/shard_map/all_to_all | solution.py:190
  83.0 0.6 fusion.3
  83.6 0.0 copy-done.3
  83.6 0.6 fusion.2
  84.2 0.6 iota_xor_fusion
  84.8 0.6 iota_xor_fusion.1
  85.5 0.1 iota_compare_fusion
  85.5 0.0 copy-done.2
  85.5 0.1 select_reduce_fusion.1
  85.6 0.6 broadcast_subtract_fusion.1
  86.3 0.1 constant_dynamic-slice_fusion.1
  86.3 0.2 select_reduce_fusion.3
  86.5 0.1 fusion
  86.6 0.1 constant_dynamic-slice_fusion
  86.7 0.1 fusion.1
  86.8 0.6 broadcast_subtract_fusion
  87.4 0.1 add_divide_fusion.factor_ref
  87.5 23.9 %all-to-all-done.2 = f32[64,32,128]{2,1,0:T(8,128)S(1)} async-done(((f32[64,32,128]{2,1,0:T(8,128)}), f32[64,32,128]{2,1,0:T(8,128)S(1)}, u32[]{:S(2)}, u32[]{:S(2)}) %all-to-all-start.2) | async-done | bytes 1048608 | tf_op jit(solution)/shard_map/all_to_all | solution.py:190
  111.4 0.7 finish.1
Async XLA Ops:
  16.6 35.6 %copy-start = (s32[64]{0:T(128)S(1)}, s32[64]{0:T(128)}, u32[]{:S(2)}) copy-start(s32[64]{0:T(128)} %occ_ref.1) | copy-start | bytes 772
  16.6 35.6 %copy-start.1 = (s32[8]{0:T(128)S(1)}, s32[8]{0:T(128)}, u32[]{:S(2)}) copy-start(s32[8]{0:T(128)} %count_ref.1) | copy-start | bytes 100
  16.6 35.5 %all-to-all-start.1 = ((f32[8,512,128]{2,1,0:T(8,128)}), f32[8,512,128]{2,1,0:T(8,128)S(1)}, u32[]{:S(2)}, u32[]{:S(2)}) async-start(f32[8,512,128]{2,1,0:T(8,128)} %param.7), calls=%async_computation.1 | async-start | bytes 4194304 | tf_op jit(solution)/shard_map/all_to_all | solution.py:181
  21.3 9.6 %collective-permute-start = (f32[8,16,512]{2,1,0:T(8,128)S(1)}, f32[8,16,512]{2,1,0:T(8,128)S(1)}, u32[]{:S(2)}, u32[]{:S(2)}) collective-permute-start(f32[8,16,512]{2,1,0:T(8,128)S(1)} %all_to_all.15.refs_0_), channel_id=1, source_target_pairs={{0,112},{1,113},{2,114},{3,115},{4,116},{5,117},{6,118},{7,119},{8... | collective-permute-start | bytes 786440 | tf_op jit(solution)/shard_map/ppermute | solution.py:22
  23.2 16.5 %collective-permute-start.1 = (f32[8,16,512]{2,1,0:T(8,128)S(1)}, f32[8,16,512]{2,1,0:T(8,128)S(1)}, u32[]{:S(2)}, u32[]{:S(2)}) collective-permute-start(f32[8,16,512]{2,1,0:T(8,128)S(1)} %all_to_all.15.refs_0_), channel_id=1, source_target_pairs={{0,16},{1,17},{2,18},{3,19},{4,20},{5,21},{6,22},{7,23},{8,24},{9,... | collective-permute-start | bytes 786440 | tf_op jit(solution)/shard_map/ppermute | solution.py:22
  26.6 19.2 %collective-permute-start.2 = (f32[8,16,512]{2,1,0:T(8,128)S(1)}, f32[8,16,512]{2,1,0:T(8,128)S(1)}, u32[]{:S(2)}, u32[]{:S(2)}) collective-permute-start(f32[8,16,512]{2,1,0:T(8,128)S(1)} %all_to_all.15.refs_0_), channel_id=1, source_target_pairs={{0,64},{1,65},{2,66},{3,67},{4,68},{5,69},{6,70},{7,71},{8,72},{9,... | collective-permute-start | bytes 786440 | tf_op jit(solution)/shard_map/ppermute | solution.py:22
  46.9 15.2 %collective-permute-start.3 = (f32[16,16,512]{2,1,0:T(8,128)}, f32[16,16,512]{2,1,0:T(8,128)}, u32[]{:S(2)}, u32[]{:S(2)}) collective-permute-start(f32[16,16,512]{2,1,0:T(8,128)} %get-tuple-element.20), channel_id=1, source_target_pairs={{0,112},{1,113},{2,114},{3,115},{4,116},{5,117},{6,118},{7,119},{8... | collective-permute-start | bytes 1572872 | tf_op jit(solution)/shard_map/ppermute | solution.py:22
  49.6 15.3 %collective-permute-start.4 = (f32[16,16,512]{2,1,0:T(8,128)}, f32[16,16,512]{2,1,0:T(8,128)}, u32[]{:S(2)}, u32[]{:S(2)}) collective-permute-start(f32[16,16,512]{2,1,0:T(8,128)} %get-tuple-element.19), channel_id=1, source_target_pairs={{0,16},{1,17},{2,18},{3,19},{4,20},{5,21},{6,22},{7,23},{8,24},{9,... | collective-permute-start | bytes 1572872 | tf_op jit(solution)/shard_map/ppermute | solution.py:22
  68.0 15.6 %copy-start.3 = (f32[64]{0:T(128)S(1)}, f32[64]{0:T(128)}, u32[]{:S(2)}) copy-start(f32[64]{0:T(128)} %param.8) | copy-start | bytes 772
  68.0 17.6 %copy-start.2 = (f32[8,128]{1,0:T(8,128)S(1)}, f32[8,128]{1,0:T(8,128)}, u32[]{:S(2)}) copy-start(f32[8,128]{1,0:T(8,128)} %param.9) | copy-start | bytes 12292
  68.0 43.5 %all-to-all-start.2 = ((f32[64,32,128]{2,1,0:T(8,128)}), f32[64,32,128]{2,1,0:T(8,128)S(1)}, u32[]{:S(2)}, u32[]{:S(2)}) async-start(f32[64,32,128]{2,1,0:T(8,128)} %bitcast), calls=%async_computation.2 | async-start | bytes 2097152 | tf_op jit(solution)/shard_map/all_to_all | solution.py:190
